TPU v7x, 256 devices: a whole 4x4x8 slice. The times are simulated.
256 devices in a mesh: beam: 2 (over core), tx: 8 (over y, x_hi), ty: 8 (over z), dom: 2 (over x_lo).
Axes of the slice: x: 4 (x_hi: 2, x_lo: 2; x = x_hi * 2 + x_lo), y: 4, z: 8, core: 2. Of those that a mesh axis runs over, the one named last changes fastest.
Arguments:
- cell_row: int32 [2, 2097152], P('beam', ('tx', 'ty', 'dom')), may hold values from 0 to 254
- cell_col: int32 [2, 2097152], P('beam', ('tx', 'ty', 'dom')), may hold values from 0 to 254
- weights: float32 [2, 2097152], P('beam', ('tx', 'ty', 'dom')), may hold values from -6 to 6
- momenta: float32 [2, 2, 2097152], P('beam', None, ('tx', 'ty', 'dom')), may hold values from -6 to 6
Outputs:
- kicked: float32 [2, 2, 2097152], P('beam', None, ('tx', 'ty', 'dom'))
Inputs may be any that keep to these rules, and one draw needn't show every extreme that they name: cell_row is a row within the tile of 256 rows that holds the macroparticle, which lies on a device of that tile; its cloud also covers the next row. cell_col is a column within the tile of 256 columns that holds the macroparticle; its cloud also covers the next column.
All inputs are finite; a program needn't handle non-finite values.
Results may differ from a plain program's by a relative error of at most 0.00005.
Values sent between devices are 32-bit elements; how exact they have to be, the bound alone decides.
A program may use at most 64 MiB of HBM per device.

v0:
```python
import jax
import jax.numpy as jnp
from jax import lax
from jax.sharding import PartitionSpec as P

GRID = 2048


highest = lax.Precision.HIGHEST
kick_gain = 2.0
block_rows = 1024


def partner(block, axis, stride):
    count = lax.axis_size(axis)
    route = []
    for low in range(count):
        high = low | 1 << stride
        if high != low and high < count:
            route += [(low, high), (high, low)]
    return lax.ppermute(block, axis, route)


def phase_angles(position, wavenum, points):
    period = 2 * (points + 1)
    phase_idx = (position + 1) * (wavenum + 1) % period
    return jnp.pi * phase_idx.astype(jnp.float32) / (points + 1)


def basis(position, wavenum, points):
    angles = phase_angles(position, wavenum, points)
    scaling = jnp.sqrt(jnp.float32(2.0) / (points + 1))
    return scaling * jnp.sin(angles)


def paired_tables(position, wavenum, points):
    angles = phase_angles(position, wavenum, points)
    scaling = jnp.sqrt(jnp.float32(2.0) / (points + 1))
    wavenumber = jnp.pi * (wavenum + 1).astype(jnp.float32) / (points + 1)
    return (scaling * jnp.sin(angles), -scaling * wavenumber * jnp.cos(angles))


def eigen_value(wavenum, points):
    halfsin = jnp.sin(jnp.pi * (wavenum + 1).astype(jnp.float32) / (2 * (points + 1)))
    return 4.0 * halfsin * halfsin


def green(row_modes, col_modes, points):
    return 1.0 / (eigen_value(row_modes, points) + eigen_value(col_modes, points))


def matmul(left, right):
    return jnp.dot(left, right, precision=highest, preferred_element_type=jnp.float32)


def shards(cell_row, cell_col, weights, momenta):
    tile_rows = GRID // lax.axis_size("tx")
    tile_cols = GRID // lax.axis_size("ty")
    share_cols = tile_cols // lax.axis_size("dom")
    count = cell_row.shape[1]
    step_rows = min(block_rows, count)
    turns = count // step_rows
    row_start = lax.axis_index("tx") * tile_rows
    col_group = lax.axis_index("ty") * lax.axis_size("dom") + lax.axis_index("dom")
    my_rows = row_start + jnp.arange(tile_rows, dtype=jnp.int32)
    my_cols = col_group * share_cols + jnp.arange(share_cols, dtype=jnp.int32)
    row_cells = jnp.arange(tile_rows, dtype=jnp.int32)
    col_cells = jnp.arange(tile_cols, dtype=jnp.int32)

    def spread(step_no):
        offset = step_no * step_rows
        rows_here = lax.dynamic_slice_in_dim(cell_row[0], offset, step_rows)
        cols_here = lax.dynamic_slice_in_dim(cell_col[0], offset, step_rows)
        row_w = 0.75 * (rows_here[:, None] == row_cells[None, :]).astype(jnp.float32) + 0.25 * (
            rows_here[:, None] + 1 == row_cells[None, :]
        ).astype(jnp.float32)
        col_w = 0.625 * (cols_here[:, None] == col_cells[None, :]).astype(jnp.float32) + 0.375 * (
            cols_here[:, None] + 1 == col_cells[None, :]
        ).astype(jnp.float32)
        return (row_w, col_w, offset)

    def deposit(step_no, running):
        row_w, col_w, offset = spread(step_no)
        charges = lax.dynamic_slice_in_dim(weights[0], offset, step_rows)
        return running + lax.dot_general(
            row_w,
            col_w * charges[:, None],
            (((0,), (0,)), ((), ())),
            precision=highest,
            preferred_element_type=jnp.float32,
        )

    tile_charge = lax.fori_loop(0, turns, deposit, jnp.zeros((tile_rows, tile_cols), jnp.float32))
    charge = lax.psum_scatter(tile_charge, "dom", scatter_dimension=1, tiled=True)
    segment = lax.all_gather(charge, "tx", axis=0, tiled=True)
    wave_in = jnp.arange(segment.shape[0], dtype=jnp.int32)
    row_done = matmul(basis(my_rows[:, None], wave_in[None, :], GRID), segment)
    segment = lax.all_gather(row_done, ("ty", "dom"), axis=1, tiled=True)
    positions = jnp.arange(segment.shape[1], dtype=jnp.int32)
    spectrum = matmul(segment, basis(positions[:, None], my_cols[None, :], GRID))
    potential_hat = green(my_rows[:, None], my_cols[None, :], GRID) * spectrum
    segment = lax.all_gather(potential_hat, ("ty", "dom"), axis=1, tiled=True)
    wave_in = jnp.arange(segment.shape[1], dtype=jnp.int32)
    sine_part, slope_part = paired_tables(my_cols[None, :], wave_in[:, None], GRID)
    along = matmul(segment, sine_part)
    across = matmul(segment, slope_part)
    pieces = (
        lax.all_gather(along, "tx", axis=0, tiled=True),
        lax.all_gather(across, "tx", axis=0, tiled=True),
    )
    wave_in = jnp.arange(pieces[0].shape[0], dtype=jnp.int32)
    sine_part, slope_part = paired_tables(my_rows[:, None], wave_in[None, :], GRID)
    field_x = matmul(slope_part, pieces[0])
    field_y = matmul(sine_part, pieces[1])
    stacked = jnp.stack([field_x, field_y])
    stacked = partner(stacked, "beam", 0)
    full_field = lax.all_gather(stacked, "dom", axis=2, tiled=True)

    def sample(step_no, kicks):
        row_w, col_w, offset = spread(step_no)
        near_x = matmul(row_w, full_field[0])
        near_y = matmul(row_w, full_field[1])
        paired = jnp.stack([jnp.sum(near_x * col_w, axis=1), jnp.sum(near_y * col_w, axis=1)])
        return lax.dynamic_update_slice_in_dim(kicks, paired, offset, 1)

    kicks = lax.fori_loop(0, turns, sample, jnp.zeros((2, count), jnp.float32))
    return momenta + kick_gain * kicks[None]


def solution(mesh):
    placed = (
        P("beam", ("tx", "ty", "dom")),
        P("beam", ("tx", "ty", "dom")),
        P("beam", ("tx", "ty", "dom")),
        P("beam", None, ("tx", "ty", "dom")),
    )
    return jax.shard_map(
        shards,
        mesh=mesh,
        in_specs=placed,
        out_specs=P("beam", None, ("tx", "ty", "dom")),
        check_vma=False,
    )
```

profile of v0, /device:TPU:4, one launch (start us, length us, event | category | flops | bytes accessed | tf_op | source)
XLA Modules:
  0.0 535.0 jit_solution(16210030725622767847)
XLA Ops:
  6.5 64.5 %while.33 = (s32[]{:T(128)}, f32[256,256]{1,0:T(8,128)S(1)}, s32[1,16384]{1,0:T(1,128)}, s32[1,16384]{1,0:T(1,128)}, f32[1,16384]{1,0:T(1,128)}, /*index=5*/s32[]{:T(128)}, s32[]{:T(128)}, s32[]{:T(128)}, s32[]{:T(128)}) while((s32[]{:T(128)}, f32[256,256]{1,0:T(8,128)S(1)}, s32[1,16384]{1,0:T(1,128)}, ...), condition=%wide.region_1.0_spmd.clone.clone, body=%wide.region_0.0_spmd.clone.clone.sunk | while | flops 808323072 | bytes 585893 | solution.py:93
  7.9 2.6 convolution_add_fusion.2
  12.0 2.6 convolution_add_fusion.2
  16.0 2.6 convolution_add_fusion.2
  20.0 2.6 convolution_add_fusion.2
  24.1 2.6 convolution_add_fusion.2
  28.1 2.6 convolution_add_fusion.2
  32.1 2.6 convolution_add_fusion.2
  36.2 2.6 convolution_add_fusion.2
  40.2 2.6 convolution_add_fusion.2
  44.2 2.6 convolution_add_fusion.2
  48.3 2.6 convolution_add_fusion.2
  52.3 2.6 convolution_add_fusion.2
  56.3 2.6 convolution_add_fusion.2
  60.4 2.6 convolution_add_fusion.2
  64.4 2.6 convolution_add_fusion.2
  68.4 2.6 convolution_add_fusion.2
  71.8 19.5 %reduce-scatter.2.cloned.1.call-done = f32[256,128]{1,0:T(8,128)} async-done(((f32[256,256]{1,0:T(8,128)}), f32[256,128]{1,0:T(8,128)}) %reduce-scatter.2.cloned.1.call-update) | async-done | bytes 131088 | tf_op jit(solution)/shard_map/reduce_scatter | solution.py:94
  91.5 53.0 %all-gather.6.cloned.1.call-done = f32[2048,128]{1,0:T(8,128)} async-done(((f32[256,128]{1,0:T(8,128)}), f32[2048,128]{1,0:T(8,128)}) %all-gather.6.cloned.1.call-update) | async-done | bytes 1048592 | tf_op jit(solution)/shard_map/all_gather | solution.py:95
  144.5 11.7 %fusion.58 = f32[256,128]{1,0:T(8,128)} fusion(f32[2048,128]{1,0:T(8,128)} %all-gather.6.cloned.1.call-done, s32[2048]{0:T(1024)S(1)} %iota_add_fusion, s32[256]{0:T(256)S(1)} %add_add_fusion), kind=kOutput, calls=%fused_computation.81 | convolution fusion | flops 810549248 | bytes 1188864 | tf_op jit(solution)/shard_map/dot_general | solution.py:53
  156.6 81.5 %all-gather.8.cloned.1.call-done = f32[256,2048]{1,0:T(8,128)} async-done(((f32[256,128]{1,0:T(8,128)}), f32[256,2048]{1,0:T(8,128)}) %all-gather.8.cloned.1.call-update) | async-done | bytes 2097168 | tf_op jit(solution)/shard_map/all_gather | solution.py:98
  238.1 8.0 %convolution_multiply_fusion.2 = f32[256,128]{1,0:T(8,128)} fusion(f32[256,2048]{1,0:T(8,128)} %all-gather.8.cloned.1.call-done, s32[128]{0:T(128)S(1)} %add_add_fusion.1, s32[2048]{0:T(1024)S(1)} %iota_add_fusion, f32[128]{0:T(128)S(1)} %multiply_multiply_fusion.1, f32[256]{0:T(256)S(1)} %multiply_multiply_fusion), kind=kOutput, calls=%fused_computation.85 | convolution fusion | flops 808026112 | bytes 2238464 | tf_op jit(solution)/shard_map/dot_general | solution.py:53
  246.2 83.7 %all-gather.10.cloned.1.call-done = f32[256,2048]{1,0:T(8,128)} async-done(((f32[256,128]{1,0:T(8,128)}), f32[256,2048]{1,0:T(8,128)}) %all-gather.10.cloned.1.call-update) | async-done | bytes 2097168 | tf_op jit(solution)/shard_map/all_gather | solution.py:102
  329.9 8.2 %fusion.90 = f32[256,128]{1,0:T(8,128)} fusion(f32[256,2048]{1,0:T(8,128)} %all-gather.10.cloned.1.call-done, s32[128]{0:T(128)S(1)} %add_add_fusion.1, s32[2048]{0:T(1024)S(1)} %iota_add_fusion), kind=kOutput, calls=%fused_computation.111 | convolution fusion | flops 807927808 | bytes 2236928 | tf_op jit(solution)/shard_map/dot_general | solution.py:53
  338.7 6.4 %fusion.65 = f32[256,128]{1,0:T(8,128)} fusion(f32[256,2048]{1,0:T(8,128)S(1)} %copy-done.2, f32[2048]{0:T(1024)S(1)} %convert_multiply_fusion, s32[128]{0:T(128)S(1)} %add_add_fusion.1, s32[2048]{0:T(1024)S(1)} %iota_add_fusion), kind=kOutput, calls=%fused_computation.88 | convolution fusion | flops 807927808 | bytes 2245120 | tf_op jit(solution)/shard_map/dot_general | solution.py:53
  345.1 45.3 %all-gather.12.cloned.1.call-done = f32[2048,128]{1,0:T(8,128)} async-done(((f32[256,128]{1,0:T(8,128)}), f32[2048,128]{1,0:T(8,128)}) %all-gather.12.cloned.1.call-update) | async-done | bytes 1048592 | tf_op jit(solution)/shard_map/all_gather | solution.py:108
  390.4 11.1 %fusion.60 = f32[1,256,128]{2,1,0:T(8,128)S(1)} fusion(f32[2048,128]{1,0:T(8,128)} %all-gather.12.cloned.1.call-done, s32[2048]{0:T(1024)S(1)} %iota_add_fusion, s32[256]{0:T(256)S(1)} %add_add_fusion, f32[2048]{0:T(1024)S(1)} %convert_multiply_fusion), kind=kOutput, calls=%fused_computation.84 | convolution fusion | flops 810549248 | bytes 1197056 | tf_op jit(solution)/shard_map/dot_general | solution.py:53
  401.5 42.0 %all-gather.14.cloned.1.call-done = f32[2048,128]{1,0:T(8,128)} async-done(((f32[256,128]{1,0:T(8,128)}), f32[2048,128]{1,0:T(8,128)}) %all-gather.14.cloned.1.call-update) | async-done | bytes 1048592 | tf_op jit(solution)/shard_map/all_gather | solution.py:109
  443.5 11.2 %fusion.59 = f32[1,256,128]{2,1,0:T(8,128)S(1)} fusion(f32[2048,128]{1,0:T(8,128)} %all-gather.14.cloned.1.call-done, s32[2048]{0:T(1024)S(1)} %iota_add_fusion, s32[256]{0:T(256)S(1)} %add_add_fusion), kind=kOutput, calls=%fused_computation.83 | convolution fusion | flops 810549248 | bytes 1188864 | tf_op jit(solution)/shard_map/dot_general | solution.py:53
  456.4 9.3 %all_gather.23 = f32[2,256,256]{2,1,0:T(8,128)S(1)} all-gather(f32[2,256,128]{2,1,0:T(8,128)S(1)} %collective-permute-done), channel_id=1, replica_groups=mesh['beam'=2,'tx'=8,'ty'=8,'dom'=2] {'dom'}, dimensions={2}, use_global_device_ids=true | all-gather | bytes 786432 | tf_op jit(solution)/shard_map/all_gather | solution.py:117
  465.8 61.4 %while.32 = (s32[]{:T(128)}, f32[2,16384]{1,0:T(2,128)S(1)}, s32[1,16384]{1,0:T(1,128)}, f32[2,256,256]{2,1,0:T(8,128)S(1)}, s32[1,16384]{1,0:T(1,128)}, /*index=5*/s32[]{:T(128)}, s32[]{:T(128)}, s32[]{:T(128)}, s32[]{:T(128)}) while((s32[]{:T(128)}, f32[2,16384]{1,0:T(2,128)S(1)}, s32[1,16384]{1,0:T(1,128)}, ...), condition=%wide.region_6.7_spmd.clone.clone, body=%wide.region_3.6_spmd.clone.clone.sunk | while | flops 1616906240 | bytes 614547 | solution.py:126
  468.1 1.5 fusion.145
  471.9 1.5 fusion.145
  475.8 1.5 fusion.145
  479.6 1.5 fusion.145
  483.4 1.5 fusion.145
  487.3 1.5 fusion.145
  491.1 1.5 fusion.145
  494.9 1.5 fusion.145
  498.8 1.5 fusion.145
  501.1 1.5 fusion.146
  502.6 1.5 fusion.145
  506.4 1.5 fusion.145
  510.3 1.5 fusion.145
  514.1 1.5 fusion.145
  518.0 1.5 fusion.145
  521.8 1.5 fusion.145
  525.6 1.5 fusion.145
  (173 shorter events, 61.6 us)
Async XLA Ops:
  6.5 84.7 %reduce-scatter.2.cloned.1.call-start = ((), (), s32[]{:S(2)}) async-start(), calls=%async_computation.1 | async-start | bytes 393216 | tf_op jit(solution)/shard_map/reduce_scatter | solution.py:94
  71.0 0.7 copy-start
  71.8 72.8 %all-gather.6.cloned.1.call-start = ((), (), s32[]{:S(2)}) async-start(), calls=%async_computation.2 | async-start | bytes 1179648 | tf_op jit(solution)/shard_map/all_gather | solution.py:95
  91.3 146.8 %all-gather.8.cloned.1.call-start = ((), (), s32[]{:S(2)}) async-start(), calls=%async_computation.3 | async-start | bytes 2228224 | tf_op jit(solution)/shard_map/all_gather | solution.py:98
  156.2 173.7 %all-gather.10.cloned.1.call-start = ((), (), s32[]{:S(2)}) async-start(), calls=%async_computation.4 | async-start | bytes 2228224 | tf_op jit(solution)/shard_map/all_gather | solution.py:102
  246.2 144.3 %all-gather.12.cloned.1.call-start = ((), (), s32[]{:S(2)}) async-start(), calls=%async_computation.5 | async-start | bytes 1179648 | tf_op jit(solution)/shard_map/all_gather | solution.py:108
  329.9 8.7 %copy-start.2 = (f32[256,2048]{1,0:T(8,128)S(1)}, f32[256,2048]{1,0:T(8,128)}, u32[]{:S(2)}) copy-start(f32[256,2048]{1,0:T(8,128)} %all-gather.10.cloned.1.call-done) | copy-start | bytes 6291460
  338.1 105.4 %all-gather.14.cloned.1.call-start = ((), (), s32[]{:S(2)}) async-start(), calls=%async_computation.6 | async-start | bytes 1179648 | tf_op jit(solution)/shard_map/all_gather | solution.py:109
  454.8 1.6 collective-permute-start
  465.8 61.4 %copy-start.1 = (f32[1,2,16384]{2,1,0:T(2,128)S(1)}, f32[1,2,16384]{2,1,0:T(2,128)}, u32[]{:S(2)}) copy-start(f32[1,2,16384]{2,1,0:T(2,128)} %param.11) | copy-start | bytes 393220
Sparse Core Ops, SparseCore 0:
  71.9 19.3 reduce-scatter.1
  94.3 50.2 all-gather.5
  156.4 81.7 all-gather.7
  246.3 83.6 all-gather.9
  338.3 52.1 all-gather.11
  393.3 50.2 all-gather.13
where the time goes:
time: 543 us; the launch traced here: 535 us
  waiting for transfers between devices  327 us (60%)
  matrix products  147 us (27%)
  local copies, waits for them, and re-layouts  34.5 us (6%)
  between operations  13.8 us (3%)
  blocking collectives  9.33 us (2%)
    dot_general x38, matrix products, matmul(): jnp.dot(left, right, precision=highest, preferred_element_type=jnp.float32)  105 us
    all_gather x1, waiting for transfers between devices, shards(): segment = lax.all_gather(potential_hat, ('ty', 'dom'), axis=1, tiled=True)  83.7 us
    all_gather x1, waiting for transfers between devices, shards(): segment = lax.all_gather(row_done, ('ty', 'dom'), axis=1, tiled=True)  81.5 us
    all_gather x1, waiting for transfers between devices, shards(): segment = lax.all_gather(charge, 'tx', axis=0, tiled=True)  53 us
    all_gather x1, waiting for transfers between devices, shards(): lax.all_gather(along, 'tx', axis=0, tiled=True)  45.3 us
    all_gather x1, waiting for transfers between devices, shards(): lax.all_gather(across, 'tx', axis=0, tiled=True)  42 us
    dot_general x16, matrix products, deposit(): lax.dot_general(row_w, col_w * charges[:, None], (((0,), (0,)), ((), ()))...  41.5 us
    dynamic_slice x32, local copies, waits for them, and re-layouts, spread(): cols_here = lax.dynamic_slice_in_dim(cell_col[0], offset, step_rows)  22.7 us
  transfers between devices with their start and end apart: 7, of which 7 were waited for; matrix products, arithmetic and copies ran while one was open for 3% of the time, Pallas kernels for 0%

commit v1 on v0

v1 whole, which is shorter than its diff:
```python
import jax
import jax.numpy as jnp
import numpy as np
from jax import lax
from jax.experimental import pallas as pl
from jax.experimental.pallas import tpu as pltpu
from jax.sharding import PartitionSpec as P

GRID = 2048
TILE = 256
BLOCKS = 8
SHARE = 16
PLANE = 16
RING = 8
HALF = 128
kick_gain = 2.0
f32 = jnp.float32
bf16 = jnp.bfloat16

COARSE_SIN, COARSE_COS, FINE_SIN, FINE_COS, CHUNK_SIN, CHUNK_COS, EIGEN, WAVE = (
    0, 16, 32, 48, 64, 72, 80, 81,
)
BASE_ROWS = 88


def base_tables():
    points = GRID + 1
    wave = np.arange(1, GRID + 1, dtype=np.int64)

    def angles(multiples):
        return np.pi * ((multiples[:, None] * wave[None, :]) % (2 * points)) / points

    coarse = angles(16 * np.arange(16, dtype=np.int64))
    fine = angles(np.arange(1, 17, dtype=np.int64))
    chunk = angles(TILE * np.arange(BLOCKS, dtype=np.int64))
    eigen = 4.0 * np.sin(np.pi * wave / (2 * points)) ** 2
    rows = np.zeros((BASE_ROWS, GRID))
    rows[0:80] = np.concatenate(
        [np.sin(coarse), np.cos(coarse), np.sin(fine), np.cos(fine), np.sin(chunk), np.cos(chunk)]
    )
    rows[EIGEN] = eigen
    rows[WAVE] = np.pi * wave / points
    blocks = rows.reshape(BASE_ROWS, BLOCKS, TILE).transpose(1, 0, 2)
    return np.ascontiguousarray(blocks).astype(np.float32)


def split(x):
    high = x.astype(bf16)
    low = (x - high.astype(f32)).astype(bf16)
    return high, low


def deposit_kernel(row_ref, col_ref, weight_ref, tile_ref, total):
    count = row_ref.shape[1]
    step = min(1024, count)
    total[...] = jnp.zeros_like(total)

    def body(i, carry):
        here = pl.ds(pl.multiple_of(i * step, step), step)
        cells = lax.broadcasted_iota(jnp.int32, (TILE, step), 0)
        weight = weight_ref[:, here]
        high = weight.astype(bf16).astype(f32)
        low = weight - high
        on_row = jnp.where(cells == row_ref[:, here], f32(1), f32(0)).astype(bf16)
        hit = cells == col_ref[:, here]
        on_col = jnp.concatenate(
            [
                jnp.where(hit, high, f32(0)).astype(bf16),
                jnp.where(hit, low, f32(0)).astype(bf16),
            ],
            axis=0,
        )
        total[...] += lax.dot_general(
            on_col, on_row, (((1,), (1,)), ((), ())), preferred_element_type=f32
        )
        return carry

    lax.fori_loop(0, count // step, body, 0)
    tile = total[0:TILE, :] + total[TILE : 2 * TILE, :]
    tile = 0.75 * tile + 0.25 * pltpu.roll(tile, 1, 1)
    tile_ref[...] = 0.625 * tile + 0.375 * pltpu.roll(tile, 1, 0)


def sample_kernel(row_ref, col_ref, momenta_ref, field_ref, out_ref, parts):
    count = row_ref.shape[1]
    step = min(1024, count)
    for comp in range(2):
        field = field_ref[comp]
        field = 0.75 * field + 0.25 * pltpu.roll(field, TILE - 1, 1)
        field = kick_gain * (0.625 * field + 0.375 * pltpu.roll(field, TILE - 1, 0))
        high, low = split(field)
        parts[comp * TILE : (comp + 1) * TILE, 0:TILE] = high
        parts[comp * TILE : (comp + 1) * TILE, TILE : 2 * TILE] = low

    def body(i, carry):
        here = pl.ds(pl.multiple_of(i * step, step), step)
        cells = lax.broadcasted_iota(jnp.int32, (TILE, step), 0)
        on_row = jnp.where(cells == row_ref[:, here], f32(1), f32(0)).astype(bf16)
        near = jnp.dot(
            parts[...], jnp.concatenate([on_row, on_row], axis=0), preferred_element_type=f32
        )
        hit = cells == col_ref[:, here]
        for comp in range(2):
            kick = jnp.sum(
                jnp.where(hit, near[comp * TILE : (comp + 1) * TILE], f32(0)),
                axis=0,
                keepdims=True,
            )
            out_ref[comp : comp + 1, here] = momenta_ref[comp : comp + 1, here] + kick
        return carry

    lax.fori_loop(0, count // step, body, 0)


def solve_kernel(
    tile_ref, base_ref, field_ref,
    tables, lines, charge_in, modes_out, modes_in, turned_out, spectrum_in, scaled,
    column_out, column_in, back_out, back_in, field_out,
    send_a, recv_a, send_b, recv_b, send_z, recv_z, send_c, recv_c, send_p, recv_p, send_d, recv_d,
):
    beam, tx = lax.axis_index("beam"), lax.axis_index("tx")
    ty, dom = lax.axis_index("ty"), lax.axis_index("dom")
    here = tx * 2 + dom
    here_x, here_y = lax.rem(here, 4), lax.div(here, 4)

    def plane_peer(offset):
        x = lax.rem(here_x + lax.rem(offset, 4), 4)
        y = lax.rem(here_y + lax.div(offset, 4), 4)
        return y * 4 + x

    def plane_id(peer):
        return {"tx": lax.div(peer, 2), "dom": lax.rem(peer, 2)}

    def ring_peer(offset):
        return lax.rem(ty + offset, RING)

    def each(first, last, act):
        def body(i, carry):
            act(i)
            return carry

        lax.fori_loop(first, last, body, 0)

    def copy(src, dst, send, recv, device):
        return pltpu.make_async_remote_copy(
            src_ref=src, dst_ref=dst, send_sem=send, recv_sem=recv,
            device_id=device, device_id_type=pl.DeviceIdType.MESH,
        )

    def copy_a(i):
        peer = plane_peer(i)
        return copy(
            tile_ref.at[peer], charge_in.at[dom, tx], send_a.at[i], recv_a.at[i],
            {"beam": 1 - beam, **plane_id(peer)},
        )

    def copy_b(i):
        peer = plane_peer(i)
        return copy(modes_out.at[peer], modes_in.at[here], send_b.at[i], recv_b.at[i], plane_id(peer))

    def copy_z(i):
        peer = ring_peer(i)
        return copy(turned_out.at[peer], spectrum_in.at[ty], send_z.at[i], recv_z.at[i], {"ty": peer})

    def copy_c(comp, i):
        peer = ring_peer(i)
        return copy(
            column_out.at[comp, peer], column_in.at[comp, ty],
            send_c.at[comp, i], recv_c.at[comp, i], {"ty": peer},
        )

    def copy_p(comp, i):
        peer = plane_peer(i)
        return copy(
            back_out.at[comp, peer], back_in.at[comp, here],
            send_p.at[comp, i], recv_p.at[comp, i], plane_id(peer),
        )

    def copy_d(comp, i):
        peer = plane_peer(i)
        return copy(
            field_out.at[comp, lax.div(peer, 2)], field_ref.at[comp, here],
            send_d.at[comp, i], recv_d.at[comp, i], plane_id(peer),
        )

    barrier = pltpu.get_barrier_semaphore()

    def greet(device):
        pl.semaphore_signal(
            barrier, inc=1, device_id=device, device_id_type=pl.DeviceIdType.MESH
        )

    each(0, PLANE, lambda i: greet({"beam": 1 - beam, **plane_id(plane_peer(i))}))
    each(1, PLANE, lambda i: greet(plane_id(plane_peer(i))))
    each(1, RING, lambda i: greet({"ty": ring_peer(i)}))
    pl.semaphore_wait(barrier, PLANE + PLANE - 1 + RING - 1)

    each(0, PLANE, lambda i: copy_a(i).start())

    def fill(j):
        fine_sin = base_ref[j, FINE_SIN : FINE_SIN + 16, :]
        fine_cos = base_ref[j, FINE_COS : FINE_COS + 16, :]
        for a in range(16):
            coarse_sin = base_ref[j, COARSE_SIN + a : COARSE_SIN + a + 1, :]
            coarse_cos = base_ref[j, COARSE_COS + a : COARSE_COS + a + 1, :]
            pair = (
                coarse_sin * fine_cos + coarse_cos * fine_sin,
                coarse_cos * fine_cos - coarse_sin * fine_sin,
            )
            for kind in range(2):
                high, low = split(pair[kind])
                tables[kind, j, 16 * a : 16 * a + 16, :] = high
                tables[kind, j, TILE + 16 * a : TILE + 16 * a + 16, :] = high
                tables[kind, j, 2 * TILE + 16 * a : 2 * TILE + 16 * a + 16, :] = low

    each(0, BLOCKS, fill)

    def load_lines(x):
        high, low = split(x.reshape(BLOCKS * SHARE, TILE))
        lines[:, 0:TILE] = high
        lines[:, TILE : 2 * TILE] = low
        lines[:, 2 * TILE : 3 * TILE] = high

    def transform(j, cosine):
        by_sin = jnp.dot(lines[...], tables[0, j], preferred_element_type=f32)
        by_cos = jnp.dot(lines[...], tables[1, j], preferred_element_type=f32)
        result = None
        for chunk in range(BLOCKS):
            rows = slice(SHARE * chunk, SHARE * chunk + SHARE)
            chunk_sin = base_ref[j, CHUNK_SIN + chunk : CHUNK_SIN + chunk + 1, :]
            chunk_cos = base_ref[j, CHUNK_COS + chunk : CHUNK_COS + chunk + 1, :]
            if cosine:
                term = chunk_cos * by_cos[rows] - chunk_sin * by_sin[rows]
            else:
                term = chunk_sin * by_cos[rows] + chunk_cos * by_sin[rows]
            result = term if result is None else result + term
        return result

    each(0, PLANE, lambda i: copy_a(i).wait_recv())
    load_lines(charge_in[0] + charge_in[1])

    def row_modes(j):
        modes = transform(j, False)
        modes_out[2 * j] = modes[:, 0:HALF]
        modes_out[2 * j + 1] = modes[:, HALF:TILE]

    each(0, BLOCKS, row_modes)
    each(1, PLANE, lambda i: copy_b(i).start())
    modes_in[here] = modes_out[here]
    each(1, PLANE, lambda i: copy_b(i).wait_recv())
    turned_out[...] = modes_in[...].reshape(TILE, HALF).T.reshape(RING, SHARE, TILE)
    each(1, RING, lambda i: copy_z(i).start())
    spectrum_in[ty] = turned_out[ty]

    first_mode = here * HALF + ty * SHARE
    lane = lax.broadcasted_iota(jnp.int32, (SHARE, TILE), 1)
    sublane = lax.broadcasted_iota(jnp.int32, (SHARE, TILE), 0)
    mine = lane == sublane + lax.rem(first_mode, TILE)
    my_block = lax.div(first_mode, TILE)

    def of_mine(row):
        values = base_ref[my_block, row : row + 1, :]
        return jnp.sum(jnp.where(mine, values, f32(0)), axis=1, keepdims=True)

    my_eigen, my_wave = of_mine(EIGEN), of_mine(WAVE)

    each(1, RING, lambda i: copy_z(i).wait_recv())
    load_lines(spectrum_in[...])
    scale = f32((2.0 / (GRID + 1)) ** 2)

    def column_modes(j):
        potential = transform(j, False) * scale / (my_eigen + base_ref[j, EIGEN : EIGEN + 1, :])
        scaled[0, j] = -my_wave * potential
        scaled[1, j] = -base_ref[j, WAVE : WAVE + 1, :] * potential

    each(0, BLOCKS, column_modes)

    for comp in range(2):
        load_lines(scaled[comp])

        def column_back(j, comp=comp):
            column_out[comp, j] = transform(j, comp == 1)

        each(0, BLOCKS, column_back)
        each(1, RING, lambda i, comp=comp: copy_c(comp, i).start())
        column_in[comp, ty] = column_out[comp, ty]

    for comp in range(2):
        each(1, RING, lambda i, comp=comp: copy_c(comp, i).wait_recv())
        back_out[comp] = column_in[comp].reshape(HALF, TILE).T.reshape(PLANE, SHARE, HALF)
        each(1, PLANE, lambda i, comp=comp: copy_p(comp, i).start())
        back_in[comp, here] = back_out[comp, here]

    for comp in range(2):
        each(1, PLANE, lambda i, comp=comp: copy_p(comp, i).wait_recv())
        load_lines(
            jnp.concatenate(
                [
                    jnp.concatenate([back_in[comp, 2 * j], back_in[comp, 2 * j + 1]], axis=1)
                    for j in range(BLOCKS)
                ],
                axis=0,
            )
        )

        def row_back(j, comp=comp):
            field_out[comp, j] = transform(j, comp == 0)

        each(0, BLOCKS, row_back)
        each(1, PLANE, lambda i, comp=comp: copy_d(comp, i).start())
        field_ref[comp, here] = field_out[comp, tx]

    for comp in range(2):
        each(1, PLANE, lambda i, comp=comp: copy_d(comp, i).wait_recv())
    each(0, PLANE, lambda i: copy_a(i).wait_send())
    each(1, PLANE, lambda i: copy_b(i).wait_send())
    each(1, RING, lambda i: copy_z(i).wait_send())
    for comp in range(2):
        each(1, RING, lambda i, comp=comp: copy_c(comp, i).wait_send())
        each(1, PLANE, lambda i, comp=comp: copy_p(comp, i).wait_send())
        each(1, PLANE, lambda i, comp=comp: copy_d(comp, i).wait_send())


vmem = pl.BlockSpec(memory_space=pltpu.VMEM)


def shards(cell_row, cell_col, weights, momenta):
    count = cell_row.shape[1]
    limit = 48 * 1024 * 1024
    tile = pl.pallas_call(
        deposit_kernel,
        out_shape=jax.ShapeDtypeStruct((TILE, TILE), f32),
        in_specs=[vmem] * 3,
        out_specs=vmem,
        scratch_shapes=[pltpu.VMEM((2 * TILE, TILE), f32)],
        compiler_params=pltpu.CompilerParams(vmem_limit_bytes=limit),
        name="deposit",
    )(cell_row, cell_col, weights)
    dma = pltpu.SemaphoreType.DMA
    field = pl.pallas_call(
        solve_kernel,
        out_shape=jax.ShapeDtypeStruct((2, PLANE, SHARE, TILE), f32),
        in_specs=[vmem] * 2,
        out_specs=vmem,
        scratch_shapes=[
            pltpu.VMEM((2, BLOCKS, 3 * TILE, TILE), bf16),
            pltpu.VMEM((BLOCKS * SHARE, 3 * TILE), bf16),
            pltpu.VMEM((2, BLOCKS, SHARE, TILE), f32),
            pltpu.VMEM((PLANE, SHARE, HALF), f32),
            pltpu.VMEM((PLANE, SHARE, HALF), f32),
            pltpu.VMEM((RING, SHARE, TILE), f32),
            pltpu.VMEM((RING, SHARE, TILE), f32),
            pltpu.VMEM((2, BLOCKS, SHARE, TILE), f32),
            pltpu.VMEM((2, RING, SHARE, TILE), f32),
            pltpu.VMEM((2, RING, SHARE, TILE), f32),
            pltpu.VMEM((2, PLANE, SHARE, HALF), f32),
            pltpu.VMEM((2, PLANE, SHARE, HALF), f32),
            pltpu.VMEM((2, BLOCKS, SHARE, TILE), f32),
            dma((PLANE,)), dma((PLANE,)),
            dma((PLANE,)), dma((PLANE,)),
            dma((RING,)), dma((RING,)),
            dma((2, RING)), dma((2, RING)),
            dma((2, PLANE)), dma((2, PLANE)),
            dma((2, PLANE)), dma((2, PLANE)),
        ],
        compiler_params=pltpu.CompilerParams(
            vmem_limit_bytes=limit, collective_id=0, has_side_effects=True
        ),
        name="solve",
    )(tile.reshape(PLANE, SHARE, TILE), jnp.asarray(base_tables()))
    kicked = pl.pallas_call(
        sample_kernel,
        out_shape=jax.ShapeDtypeStruct((2, count), f32),
        in_specs=[vmem] * 4,
        out_specs=vmem,
        scratch_shapes=[pltpu.VMEM((2 * TILE, 2 * TILE), bf16)],
        compiler_params=pltpu.CompilerParams(vmem_limit_bytes=limit),
        name="sample",
    )(cell_row, cell_col, momenta[0], field.reshape(2, TILE, TILE))
    return kicked[None]


def solution(mesh):
    placed = (
        P("beam", ("tx", "ty", "dom")),
        P("beam", ("tx", "ty", "dom")),
        P("beam", ("tx", "ty", "dom")),
        P("beam", None, ("tx", "ty", "dom")),
    )
    return jax.shard_map(
        shards,
        mesh=mesh,
        in_specs=placed,
        out_specs=P("beam", None, ("tx", "ty", "dom")),
        check_vma=False,
    )
```

time: 543 us -> 84.4 us (0.16); the launches traced: 535 us -> 83.7 us
  waiting for transfers between devices: 327 us -> 0 us
  matrix products: 147 us -> 0 us
  Pallas kernels: 0 us -> 80 us
  local copies, waits for them, and re-layouts: 34.5 us -> 3.63 us
  between operations: 13.8 us -> 0.05 us
  blocking collectives: 9.33 us -> 0 us
    all_gather x5 -> x0, waiting for transfers between devices: 306 us -> none  [the longest x1 83.7 us: shards(): segment = lax.all_gather(potential_hat, ('ty', 'dom'), axis=1, tiled=True)]
    dot_general x54 -> x0, matrix products: 147 us -> none  [the longest x38 105 us: matmul(): jnp.dot(left, right, precision=highest, preferred_element_type=jnp.float32)]
    pallas_call x0 -> x3, Pallas kernels: none -> 80 us  [the longest x1 57.7 us: shards(): pl.pallas_call(solve_kernel, out_shape=jax.ShapeDtypeStruct((2, PLANE, SH...]
    dynamic_slice x48 -> x0, local copies, waits for them, and re-layouts: 33.7 us -> none  [the longest x32 22.7 us: spread(): cols_here = lax.dynamic_slice_in_dim(cell_col[0], offset, step_rows)]
    reduce_scatter x1 -> x0, waiting for transfers between devices: 19.5 us -> none  [shards(): lax.psum_scatter(tile_charge, 'dom', scatter_dimension=1, tiled=True)]
    all_gather x1 -> x0, blocking collectives: 9.33 us -> none  [shards(): full_field = lax.all_gather(stacked, 'dom', axis=2, tiled=True)]
  transfers between devices with their start and end apart: 7 -> 0, of which waited for: 7 -> 0; matrix products, arithmetic and copies ran while one was open for 3% -> 0% of each run, Pallas kernels for 0% -> 0%
where the time goes in v1:
time: 84.4 us; the launch traced here: 83.7 us
  Pallas kernels  80 us (95%)
  local copies, waits for them, and re-layouts  3.63 us (4%)
    pallas_call x1, Pallas kernels, shards(): pl.pallas_call(solve_kernel, out_shape=jax.ShapeDtypeStruct((2, PLANE, SH...  57.7 us
    pallas_call x1, Pallas kernels, shards(): pl.pallas_call(sample_kernel, out_shape=jax.ShapeDtypeStruct((2, count),...  14 us
    pallas_call x1, Pallas kernels, shards(): pl.pallas_call(deposit_kernel, out_shape=jax.ShapeDtypeStruct((TILE, TILE...  8.35 us
    unnamed x14, local copies, waits for them, and re-layouts  3.63 us

profile of v1, /device:TPU:4, one launch (start us, length us, event | category | flops | bytes accessed | tf_op | source)
XLA Modules:
  0.0 83.7 jit_solution(14029928185103812066)
XLA Ops:
  0.0 0.0 copy-start.1
  0.0 0.8 %copy-done.1 = s32[1,16384]{1,0:T(1,128)S(1)} copy-done((s32[1,16384]{1,0:T(1,128)S(1)}, s32[1,16384]{1,0:T(1,128)}, u32[]{:S(2)}) %copy-start.1) | copy-done | bytes 65560
  0.8 0.0 copy-start.3
  0.8 0.8 %copy-done.3 = s32[1,16384]{1,0:T(1,128)S(1)} copy-done((s32[1,16384]{1,0:T(1,128)S(1)}, s32[1,16384]{1,0:T(1,128)}, u32[]{:S(2)}) %copy-start.3) | copy-done | bytes 65560
  1.7 0.0 copy-start.6
  1.7 0.8 %copy-done.6 = f32[1,16384]{1,0:T(1,128)S(1)} copy-done((f32[1,16384]{1,0:T(1,128)S(1)}, f32[1,16384]{1,0:T(1,128)}, u32[]{:S(2)}) %copy-start.6) | copy-done | bytes 65560
  2.5 8.4 %deposit.1 = f32[256,256]{1,0:T(8,128)S(1)} custom-call(s32[1,16384]{1,0:T(1,128)S(1)} %copy-done.1, s32[1,16384]{1,0:T(1,128)S(1)} %copy-done.3, f32[1,16384]{1,0:T(1,128)S(1)} %copy-done.6), custom_call_target="tpu_custom_call" | custom-call | tf_op jit(solution)/shard_map/deposit/pallas_call | solution.py:330
  10.9 0.0 copy-start
  10.9 1.1 %copy-done = f32[8,88,256]{2,1,0:T(8,128)S(1)} copy-done((f32[8,88,256]{2,1,0:T(8,128)S(1)}, f32[8,88,256]{2,1,0:T(8,128)}, u32[]{:S(2)}) %copy-start) | copy-done | bytes 720920
  12.0 0.0 copy-start.2
  12.0 0.0 copy-start.4
  12.0 0.0 copy-start.5
  12.0 57.7 %solve.1 = f32[2,16,16,256]{3,2,1,0:T(8,128)S(1)} custom-call(f32[16,16,256]{2,1,0:T(8,128)S(1)} %bitcast.5, f32[8,88,256]{2,1,0:T(8,128)S(1)} %copy-done), custom_call_target="tpu_custom_call" | custom-call | tf_op jit(solution)/shard_map/solve/pallas_call | solution.py:340
  69.7 0.0 copy-done.2
  69.7 0.0 copy-done.4
  69.7 0.0 copy-done.5
  69.7 14.0 %sample.1 = f32[2,16384]{1,0:T(2,128)} custom-call(s32[1,16384]{1,0:T(1,128)S(1)} %copy-done.2, s32[1,16384]{1,0:T(1,128)S(1)} %copy-done.4, f32[2,16384]{1,0:T(2,128)S(1)} %bitcast.6, f32[2,256,256]{2,1,0:T(8,128)S(1)} %bitcast.4), custom_call_target="tpu_custom_call" | custom-call | tf_op jit(solution)/shard_map/sample/pallas_call | solution.py:371
Async XLA Ops:
  0.0 0.8 %copy-start.1 = (s32[1,16384]{1,0:T(1,128)S(1)}, s32[1,16384]{1,0:T(1,128)}, u32[]{:S(2)}) copy-start(s32[1,16384]{1,0:T(1,128)} %row_ref.3) | copy-start | bytes 196612
  0.8 0.8 %copy-start.3 = (s32[1,16384]{1,0:T(1,128)S(1)}, s32[1,16384]{1,0:T(1,128)}, u32[]{:S(2)}) copy-start(s32[1,16384]{1,0:T(1,128)} %col_ref.3) | copy-start | bytes 196612
  1.7 0.8 %copy-start.6 = (f32[1,16384]{1,0:T(1,128)S(1)}, f32[1,16384]{1,0:T(1,128)}, u32[]{:S(2)}) copy-start(f32[1,16384]{1,0:T(1,128)} %weight_ref.1) | copy-start | bytes 196612
  10.9 1.1 %copy-start = (f32[8,88,256]{2,1,0:T(8,128)S(1)}, f32[8,88,256]{2,1,0:T(8,128)}, u32[]{:S(2)}) copy-start(f32[8,88,256]{2,1,0:T(8,128)} %constant.2.clone.base_ref) | copy-start | bytes 2162692
  12.0 57.7 %copy-start.2 = (s32[1,16384]{1,0:T(1,128)S(1)}, s32[1,16384]{1,0:T(1,128)}, u32[]{:S(2)}) copy-start(s32[1,16384]{1,0:T(1,128)} %row_ref.3) | copy-start | bytes 196612
  12.0 57.7 %copy-start.4 = (s32[1,16384]{1,0:T(1,128)S(1)}, s32[1,16384]{1,0:T(1,128)}, u32[]{:S(2)}) copy-start(s32[1,16384]{1,0:T(1,128)} %col_ref.3) | copy-start | bytes 196612
  12.0 57.7 %copy-start.5 = (f32[1,2,16384]{2,1,0:T(2,128)S(1)}, f32[1,2,16384]{2,1,0:T(2,128)}, u32[]{:S(2)}) copy-start(f32[1,2,16384]{2,1,0:T(2,128)} %param.8) | copy-start | bytes 393220

commit v2 on v1

v2 whole, which is shorter than its diff:
```python
import jax
import jax.numpy as jnp
import numpy as np
from jax import lax
from jax.experimental import pallas as pl
from jax.experimental.pallas import tpu as pltpu
from jax.sharding import PartitionSpec as P

GRID = 2048
TILE = 256
BLOCKS = 8
SHARE = 16
PLANE = 16
RING = 8
HALF = 128
DEPOSIT_STEP = 4096
SAMPLE_STEP = 2048
kick_gain = 2.0
f32 = jnp.float32
bf16 = jnp.bfloat16

COARSE_SIN, COARSE_COS, FINE_SIN, FINE_COS, CENTRE_SIN, CENTRE_COS, EIGEN, WAVE = (
    0, 8, 16, 32, 48, 56, 64, 65,
)
BASE_ROWS = 72


def base_tables():
    points = GRID + 1
    wave = np.arange(1, GRID + 1, dtype=np.int64)

    def angles(doubled):
        doubled = np.asarray(doubled, dtype=np.int64)
        return np.pi * ((doubled[:, None] * wave[None, :]) % (4 * points)) / (2 * points)

    coarse = angles(32 * np.arange(8))
    fine = angles(2 * np.arange(16) + 1)
    centre = angles(2 * TILE * np.arange(BLOCKS) + TILE + 1)
    rows = np.zeros((BASE_ROWS, GRID))
    rows[0:64] = np.concatenate(
        [np.sin(coarse), np.cos(coarse), np.sin(fine), np.cos(fine), np.sin(centre), np.cos(centre)]
    )
    rows[EIGEN] = 4.0 * np.sin(np.pi * wave / (2 * points)) ** 2
    rows[WAVE] = np.pi * wave / points
    blocks = rows.reshape(BASE_ROWS, BLOCKS, TILE).transpose(1, 0, 2)
    return np.ascontiguousarray(blocks).astype(np.float32)


def split(x):
    high = x.astype(bf16)
    low = (x - high.astype(f32)).astype(bf16)
    return high, low


def collide_kernel(
    row_hbm, col_hbm, weight_hbm, momenta_hbm, base_hbm, out_ref,
    row_ref, col_ref, weight_ref, momenta_ref, base_ref,
    on_rows, total, tile_out, tables, even, odd, charge_in, modes_out, modes_in, turned_out,
    spectrum_in, scaled, column_out, column_in, back_out, back_in, field_out, field_in, parts,
    load, send_a, recv_a, send_b, recv_b, send_z, recv_z, send_c, recv_c, send_p, recv_p,
    send_d, recv_d,
):
    beam, tx = lax.axis_index("beam"), lax.axis_index("tx")
    ty, dom = lax.axis_index("ty"), lax.axis_index("dom")
    here = tx * 2 + dom
    count = row_ref.shape[1]

    loads = [
        pltpu.make_async_copy(src, dst, load.at[i])
        for i, (src, dst) in enumerate(
            [
                (row_hbm, row_ref), (col_hbm, col_ref), (weight_hbm, weight_ref),
                (base_hbm, base_ref), (momenta_hbm, momenta_ref),
            ]
        )
    ]
    for item in loads:
        item.start()

    def each(first, last, act):
        def body(i, carry):
            act(i)
            return carry

        lax.fori_loop(first, last, body, 0)

    def plane_id(peer):
        return {"tx": lax.div(peer, 2), "dom": lax.rem(peer, 2)}

    def other_id(peer):
        return {"beam": 1 - beam, "tx": lax.div(peer, 2), "dom": lax.rem(peer, 2)}

    def ring_id(peer):
        return {"ty": peer}

    def plane_peer(i):
        return lax.rem(here + i, PLANE)

    def ring_peer(i):
        return lax.rem(ty + i, RING)

    def copy(src, dst, send, recv, device):
        return pltpu.make_async_remote_copy(
            src_ref=src, dst_ref=dst, send_sem=send, recv_sem=recv,
            device_id=device, device_id_type=pl.DeviceIdType.MESH,
        )

    def to_a(peer):
        return copy(
            tile_out.at[peer], charge_in.at[dom, tx], send_a.at[peer], recv_a.at[here],
            other_id(peer),
        )

    def from_a(peer):
        slot = charge_in.at[lax.rem(peer, 2), lax.div(peer, 2)]
        return copy(slot, slot, send_a.at[peer], recv_a.at[peer], other_id(peer))

    def to_b(peer):
        return copy(
            modes_out.at[peer], modes_in.at[here], send_b.at[peer], recv_b.at[here],
            plane_id(peer),
        )

    def from_b(peer):
        slot = modes_in.at[peer]
        return copy(slot, slot, send_b.at[peer], recv_b.at[peer], plane_id(peer))

    def to_z(peer):
        return copy(
            turned_out.at[peer], spectrum_in.at[ty], send_z.at[peer], recv_z.at[ty],
            ring_id(peer),
        )

    def from_z(peer):
        slot = spectrum_in.at[peer]
        return copy(slot, slot, send_z.at[peer], recv_z.at[peer], ring_id(peer))

    def to_c(comp, peer):
        return copy(
            column_out.at[comp, peer], column_in.at[comp, ty],
            send_c.at[comp, peer], recv_c.at[comp, ty], ring_id(peer),
        )

    def from_c(comp, peer):
        slot = column_in.at[comp, peer]
        return copy(slot, slot, send_c.at[comp, peer], recv_c.at[comp, peer], ring_id(peer))

    def to_p(comp, peer):
        return copy(
            back_out.at[comp, peer], back_in.at[comp, here],
            send_p.at[comp, peer], recv_p.at[comp, here], plane_id(peer),
        )

    def from_p(comp, peer):
        slot = back_in.at[comp, peer]
        return copy(slot, slot, send_p.at[comp, peer], recv_p.at[comp, peer], plane_id(peer))

    def to_d(comp, peer):
        return copy(
            field_out.at[comp, lax.div(peer, 2)], field_in.at[comp, here],
            send_d.at[comp, peer], recv_d.at[comp, here], plane_id(peer),
        )

    def from_d(comp, peer):
        slot = field_in.at[comp, peer]
        return copy(slot, slot, send_d.at[comp, peer], recv_d.at[comp, peer], plane_id(peer))

    barrier = pltpu.get_barrier_semaphore()

    def greet(device):
        pl.semaphore_signal(
            barrier, inc=1, device_id=device, device_id_type=pl.DeviceIdType.MESH
        )

    each(0, PLANE, lambda i: greet(other_id(plane_peer(i))))
    each(1, PLANE, lambda i: greet(plane_id(plane_peer(i))))
    each(1, RING, lambda i: greet(ring_id(ring_peer(i))))

    total[...] = jnp.zeros_like(total)
    for item in loads[0:3]:
        item.wait()
    step = min(DEPOSIT_STEP, count)

    def deposit(i):
        part = pl.ds(pl.multiple_of(i * step, step), step)
        cells = lax.broadcasted_iota(jnp.int32, (TILE, step), 0).astype(f32).astype(bf16)
        high, low = split(weight_ref[:, part])
        on_row = jnp.where(
            cells == row_ref[:, part].astype(f32).astype(bf16), bf16(1), bf16(0)
        )
        on_rows[:, part] = on_row
        hit = cells == col_ref[:, part].astype(f32).astype(bf16)
        on_col = jnp.concatenate(
            [jnp.where(hit, high, bf16(0)), jnp.where(hit, low, bf16(0))], axis=0
        )
        total[...] += lax.dot_general(
            on_col, on_row, (((1,), (1,)), ((), ())), preferred_element_type=f32
        )

    each(0, count // step, deposit)
    tile = total[0:TILE, :] + total[TILE : 2 * TILE, :]
    tile = 0.75 * tile + 0.25 * pltpu.roll(tile, 1, 1)
    tile = 0.625 * tile + 0.375 * pltpu.roll(tile, 1, 0)
    tile_out[...] = tile.reshape(PLANE, SHARE, TILE)

    pl.semaphore_wait(barrier, PLANE + PLANE - 1 + RING - 1)
    each(0, PLANE, lambda i: to_a(plane_peer(i)).start())

    loads[3].wait()

    def fill(j):
        fine_sin = base_ref[j, FINE_SIN : FINE_SIN + 16, :]
        fine_cos = base_ref[j, FINE_COS : FINE_COS + 16, :]
        for a in range(8):
            coarse_sin = base_ref[j, COARSE_SIN + a : COARSE_SIN + a + 1, :]
            coarse_cos = base_ref[j, COARSE_COS + a : COARSE_COS + a + 1, :]
            pair = (
                coarse_sin * fine_cos + coarse_cos * fine_sin,
                coarse_cos * fine_cos - coarse_sin * fine_sin,
            )
            for kind in range(2):
                high, low = split(pair[kind])
                tables[kind, j, 16 * a : 16 * a + 16, :] = high
                tables[kind, j, HALF + 16 * a : HALF + 16 * a + 16, :] = low

    each(0, BLOCKS, fill)
    even[HALF:TILE, HALF:TILE] = jnp.zeros((HALF, HALF), bf16)
    odd[HALF:TILE, HALF:TILE] = jnp.zeros((HALF, HALF), bf16)

    def load_lines(left, right):
        backward = (HALF - 1) - lax.broadcasted_iota(jnp.int32, (HALF, HALF), 1)
        left = jnp.take_along_axis(left, backward, axis=1)
        for ref, folded in ((even, right + left), (odd, right - left)):
            high, low = split(folded)
            ref[0:HALF, 0:HALF] = high
            ref[0:HALF, HALF:TILE] = high
            ref[HALF:TILE, 0:HALF] = low

    def load_chunks(x):
        x = x.reshape(BLOCKS * SHARE, TILE)
        load_lines(x[:, 0:HALF], x[:, HALF:TILE])

    def transform(j, cosine):
        by_sin = jnp.dot(odd[...], tables[0, j], preferred_element_type=f32)
        by_cos = jnp.dot(even[...], tables[1, j], preferred_element_type=f32)
        by_sin = by_sin[0:HALF] + by_sin[HALF:TILE]
        by_cos = by_cos[0:HALF] + by_cos[HALF:TILE]
        result = None
        for chunk in range(BLOCKS):
            rows = slice(SHARE * chunk, SHARE * chunk + SHARE)
            centre_sin = base_ref[j, CENTRE_SIN + chunk : CENTRE_SIN + chunk + 1, :]
            centre_cos = base_ref[j, CENTRE_COS + chunk : CENTRE_COS + chunk + 1, :]
            if cosine:
                term = centre_cos * by_cos[rows] - centre_sin * by_sin[rows]
            else:
                term = centre_sin * by_cos[rows] + centre_cos * by_sin[rows]
            result = term if result is None else result + term
        return result

    def send_plane(peer, start):
        @pl.when(peer != here)
        def _():
            start(peer)

    each(0, PLANE, lambda i: from_a(plane_peer(i)).wait_recv())
    load_chunks(charge_in[0] + charge_in[1])

    def row_modes(i):
        j = lax.rem(tx + 1 + i, BLOCKS)
        modes = transform(j, False)
        modes_out[2 * j] = modes[:, 0:HALF]
        modes_out[2 * j + 1] = modes[:, HALF:TILE]
        for peer in (2 * j, 2 * j + 1):
            send_plane(peer, lambda peer: to_b(peer).start())

    each(0, BLOCKS, row_modes)
    modes_in[here] = modes_out[here]

    first_mode = here * HALF + ty * SHARE
    lane = lax.broadcasted_iota(jnp.int32, (SHARE, TILE), 1)
    sublane = lax.broadcasted_iota(jnp.int32, (SHARE, TILE), 0)
    mine = lane == sublane + lax.rem(first_mode, TILE)
    my_block = lax.div(first_mode, TILE)

    def of_mine(row):
        values = base_ref[my_block, row : row + 1, :]
        return jnp.sum(jnp.where(mine, values, f32(0)), axis=1, keepdims=True)

    my_eigen, my_wave = of_mine(EIGEN), of_mine(WAVE)

    each(1, PLANE, lambda i: from_b(plane_peer(i)).wait_recv())
    turned_out[...] = modes_in[...].reshape(TILE, HALF).T.reshape(RING, SHARE, TILE)
    each(1, RING, lambda i: to_z(ring_peer(i)).start())
    spectrum_in[ty] = turned_out[ty]

    each(1, RING, lambda i: from_z(ring_peer(i)).wait_recv())
    load_chunks(spectrum_in[...])
    scale = f32((2.0 / (GRID + 1)) ** 2)

    def column_modes(j):
        potential = transform(j, False) * scale / (my_eigen + base_ref[j, EIGEN : EIGEN + 1, :])
        scaled[0, j] = -my_wave * potential
        scaled[1, j] = -base_ref[j, WAVE : WAVE + 1, :] * potential

    each(0, BLOCKS, column_modes)

    for comp in range(2):
        load_chunks(scaled[comp])

        def column_back(i, comp=comp):
            j = lax.rem(ty + 1 + i, BLOCKS)
            column_out[comp, j] = transform(j, comp == 1)

            @pl.when(j != ty)
            def _():
                to_c(comp, j).start()

        each(0, BLOCKS, column_back)
        column_in[comp, ty] = column_out[comp, ty]

    for comp in range(2):
        each(1, RING, lambda i, comp=comp: from_c(comp, ring_peer(i)).wait_recv())
        back_out[comp] = column_in[comp].reshape(HALF, TILE).T.reshape(PLANE, SHARE, HALF)
        each(1, PLANE, lambda i, comp=comp: to_p(comp, plane_peer(i)).start())
        back_in[comp, here] = back_out[comp, here]

    for comp in range(2):
        each(1, PLANE, lambda i, comp=comp: from_p(comp, plane_peer(i)).wait_recv())
        load_lines(
            jnp.concatenate([back_in[comp, 2 * j] for j in range(BLOCKS)], axis=0),
            jnp.concatenate([back_in[comp, 2 * j + 1] for j in range(BLOCKS)], axis=0),
        )

        def row_back(i, comp=comp):
            j = lax.rem(tx + 1 + i, BLOCKS)
            field_out[comp, j] = transform(j, comp == 0)
            for peer in (2 * j, 2 * j + 1):
                send_plane(peer, lambda peer: to_d(comp, peer).start())

        each(0, BLOCKS, row_back)
        field_in[comp, here] = field_out[comp, tx]

    loads[4].wait()
    turn = min(SAMPLE_STEP, count)
    for comp in range(2):
        each(1, PLANE, lambda i, comp=comp: from_d(comp, plane_peer(i)).wait_recv())
        field = field_in[comp].reshape(TILE, TILE)
        field = 0.75 * field + 0.25 * pltpu.roll(field, TILE - 1, 1)
        field = kick_gain * (0.625 * field + 0.375 * pltpu.roll(field, TILE - 1, 0))
        high, low = split(field)
        parts[0:TILE, :] = high
        parts[TILE : 2 * TILE, :] = low

        def sample(i, comp=comp):
            part = pl.ds(pl.multiple_of(i * turn, turn), turn)
            cells = lax.broadcasted_iota(jnp.int32, (TILE, turn), 0)
            near = jnp.dot(parts[...], on_rows[:, part], preferred_element_type=f32)
            near = near[0:TILE] + near[TILE : 2 * TILE]
            kick = jnp.sum(
                jnp.where(cells == col_ref[:, part], near, f32(0)), axis=0, keepdims=True
            )
            out_ref[comp : comp + 1, part] = momenta_ref[comp : comp + 1, part] + kick

        each(0, count // turn, sample)

    each(0, PLANE, lambda i: to_a(plane_peer(i)).wait_send())
    each(1, PLANE, lambda i: to_b(plane_peer(i)).wait_send())
    each(1, RING, lambda i: to_z(ring_peer(i)).wait_send())
    for comp in range(2):
        each(1, RING, lambda i, comp=comp: to_c(comp, ring_peer(i)).wait_send())
        each(1, PLANE, lambda i, comp=comp: to_p(comp, plane_peer(i)).wait_send())
        each(1, PLANE, lambda i, comp=comp: to_d(comp, plane_peer(i)).wait_send())


def shards(cell_row, cell_col, weights, momenta):
    count = cell_row.shape[1]
    dma = pltpu.SemaphoreType.DMA
    base = base_tables()
    kicked = pl.pallas_call(
        collide_kernel,
        out_shape=jax.ShapeDtypeStruct((2, count), f32),
        in_specs=[pl.BlockSpec(memory_space=pltpu.HBM)] * 5,
        out_specs=pl.BlockSpec(memory_space=pltpu.VMEM),
        scratch_shapes=[
            pltpu.VMEM((1, count), jnp.int32),
            pltpu.VMEM((1, count), jnp.int32),
            pltpu.VMEM((1, count), f32),
            pltpu.VMEM((2, count), f32),
            pltpu.VMEM(base.shape, f32),
            pltpu.VMEM((TILE, count), bf16),
            pltpu.VMEM((2 * TILE, TILE), f32),
            pltpu.VMEM((PLANE, SHARE, TILE), f32),
            pltpu.VMEM((2, BLOCKS, TILE, TILE), bf16),
            pltpu.VMEM((TILE, TILE), bf16),
            pltpu.VMEM((TILE, TILE), bf16),
            pltpu.VMEM((2, BLOCKS, SHARE, TILE), f32),
            pltpu.VMEM((PLANE, SHARE, HALF), f32),
            pltpu.VMEM((PLANE, SHARE, HALF), f32),
            pltpu.VMEM((RING, SHARE, TILE), f32),
            pltpu.VMEM((RING, SHARE, TILE), f32),
            pltpu.VMEM((2, BLOCKS, SHARE, TILE), f32),
            pltpu.VMEM((2, RING, SHARE, TILE), f32),
            pltpu.VMEM((2, RING, SHARE, TILE), f32),
            pltpu.VMEM((2, PLANE, SHARE, HALF), f32),
            pltpu.VMEM((2, PLANE, SHARE, HALF), f32),
            pltpu.VMEM((2, BLOCKS, SHARE, TILE), f32),
            pltpu.VMEM((2, PLANE, SHARE, TILE), f32),
            pltpu.VMEM((2 * TILE, TILE), bf16),
            dma((5,)),
            dma((PLANE,)), dma((PLANE,)),
            dma((PLANE,)), dma((PLANE,)),
            dma((RING,)), dma((RING,)),
            dma((2, RING)), dma((2, RING)),
            dma((2, PLANE)), dma((2, PLANE)),
            dma((2, PLANE)), dma((2, PLANE)),
        ],
        compiler_params=pltpu.CompilerParams(
            vmem_limit_bytes=56 * 1024 * 1024, collective_id=0, has_side_effects=True
        ),
        name="collide",
    )(cell_row, cell_col, weights, momenta[0], jnp.asarray(base))
    return kicked[None]


def solution(mesh):
    placed = (
        P("beam", ("tx", "ty", "dom")),
        P("beam", ("tx", "ty", "dom")),
        P("beam", ("tx", "ty", "dom")),
        P("beam", None, ("tx", "ty", "dom")),
    )
    return jax.shard_map(
        shards,
        mesh=mesh,
        in_specs=placed,
        out_specs=P("beam", None, ("tx", "ty", "dom")),
        check_vma=False,
    )
```

time: 84.4 us -> 66.8 us (0.79)
  Pallas kernels: 80 us -> 64.9 us
  local copies, waits for them, and re-layouts: 3.63 us -> 1.57 us
    pallas_call x3 -> x1, Pallas kernels: 80 us -> 64.9 us  [shards(): pl.pallas_call(collide_kernel, out_shape=jax.ShapeDtypeStruct((2, count),...]
    unnamed x14 -> x1, local copies, waits for them, and re-layouts: 3.63 us -> 1.57 us
where the time goes in v2:
time: 66.8 us; the launch traced here: 66.5 us
  Pallas kernels  64.9 us (97%)
  local copies, waits for them, and re-layouts  1.57 us (2%)
    pallas_call x1, Pallas kernels, shards(): pl.pallas_call(collide_kernel, out_shape=jax.ShapeDtypeStruct((2, count),...  64.9 us
    unnamed x1, local copies, waits for them, and re-layouts  1.57 us

profile of v2, /device:TPU:4, one launch (start us, length us, event | category | flops | bytes accessed | tf_op | source)
XLA Modules:
  0.0 66.5 jit_solution(1105101101786542117)
XLA Ops:
  0.0 64.9 %collide.1 = f32[2,16384]{1,0:T(2,128)} custom-call(s32[1,16384]{1,0:T(1,128)} %row_hbm.1, s32[1,16384]{1,0:T(1,128)} %col_hbm.1, f32[1,16384]{1,0:T(1,128)} %weight_hbm.1, f32[2,16384]{1,0:T(2,128)} %bitcast.3, f32[8,72,256]{2,1,0:T(8,128)} %constant.2.clone.base_hbm), custom_call_target="tpu_custom_call" | custom-call | tf_op jit(solution)/shard_map/collide/pallas_call | solution.py:379
  64.9 1.6 %copy.7 = f32[1,2,16384]{2,1,0:T(2,128)} copy(f32[1,2,16384]{2,1,0:T(2,128)} %bitcast.2) | data formatting | bytes 262144

commit v3 on v2

--- a/solution.py
+++ b/solution.py
@@ -13,8 +13,8 @@
 PLANE = 16
 RING = 8
 HALF = 128
-DEPOSIT_STEP = 4096
-SAMPLE_STEP = 2048
+DEPOSIT_STEP = 8192
+SAMPLE_STEP = 8192
 kick_gain = 2.0
 f32 = jnp.float32
 bf16 = jnp.bfloat16
@@ -23,6 +23,8 @@
     0, 8, 16, 32, 48, 56, 64, 65,
 )
 BASE_ROWS = 72
+
+EX_A, EX_B, EX_Z, EX_C, EX_P, EX_D, EXCHANGES = 0, 1, 2, 3, 5, 7, 9
 
 
 def base_tables():
@@ -53,12 +55,11 @@
 
 
 def collide_kernel(
-    row_hbm, col_hbm, weight_hbm, momenta_hbm, base_hbm, out_ref,
-    row_ref, col_ref, weight_ref, momenta_ref, base_ref,
+    row_hbm, col_hbm, weight_hbm, momenta_hbm, base_hbm, out_hbm,
+    row_ref, col_ref, weight_ref, momenta_ref, base_ref, out_ref,
     on_rows, total, tile_out, tables, even, odd, charge_in, modes_out, modes_in, turned_out,
     spectrum_in, scaled, column_out, column_in, back_out, back_in, field_out, field_in, parts,
-    load, send_a, recv_a, send_b, recv_b, send_z, recv_z, send_c, recv_c, send_p, recv_p,
-    send_d, recv_d,
+    load, sent, came,
 ):
     beam, tx = lax.axis_index("beam"), lax.axis_index("tx")
     ty, dom = lax.axis_index("ty"), lax.axis_index("dom")
@@ -99,71 +100,48 @@
     def ring_peer(i):
         return lax.rem(ty + i, RING)
 
-    def copy(src, dst, send, recv, device):
+    def copy(src, dst, exchange, device):
         return pltpu.make_async_remote_copy(
-            src_ref=src, dst_ref=dst, send_sem=send, recv_sem=recv,
+            src_ref=src, dst_ref=dst, send_sem=sent.at[exchange], recv_sem=came.at[exchange],
             device_id=device, device_id_type=pl.DeviceIdType.MESH,
         )
 
     def to_a(peer):
-        return copy(
-            tile_out.at[peer], charge_in.at[dom, tx], send_a.at[peer], recv_a.at[here],
-            other_id(peer),
-        )
-
-    def from_a(peer):
-        slot = charge_in.at[lax.rem(peer, 2), lax.div(peer, 2)]
-        return copy(slot, slot, send_a.at[peer], recv_a.at[peer], other_id(peer))
+        return copy(tile_out.at[peer], charge_in.at[dom, tx], EX_A, other_id(peer))
 
     def to_b(peer):
-        return copy(
-            modes_out.at[peer], modes_in.at[here], send_b.at[peer], recv_b.at[here],
-            plane_id(peer),
-        )
-
-    def from_b(peer):
-        slot = modes_in.at[peer]
-        return copy(slot, slot, send_b.at[peer], recv_b.at[peer], plane_id(peer))
+        return copy(modes_out.at[peer], modes_in.at[here], EX_B, plane_id(peer))
 
     def to_z(peer):
-        return copy(
-            turned_out.at[peer], spectrum_in.at[ty], send_z.at[peer], recv_z.at[ty],
-            ring_id(peer),
-        )
-
-    def from_z(peer):
-        slot = spectrum_in.at[peer]
-        return copy(slot, slot, send_z.at[peer], recv_z.at[peer], ring_id(peer))
+        return copy(turned_out.at[peer], spectrum_in.at[ty], EX_Z, ring_id(peer))
 
     def to_c(comp, peer):
         return copy(
-            column_out.at[comp, peer], column_in.at[comp, ty],
-            send_c.at[comp, peer], recv_c.at[comp, ty], ring_id(peer),
-        )
-
-    def from_c(comp, peer):
-        slot = column_in.at[comp, peer]
-        return copy(slot, slot, send_c.at[comp, peer], recv_c.at[comp, peer], ring_id(peer))
+            column_out.at[comp, peer], column_in.at[comp, ty], EX_C + comp, ring_id(peer)
+        )
 
     def to_p(comp, peer):
-        return copy(
-            back_out.at[comp, peer], back_in.at[comp, here],
-            send_p.at[comp, peer], recv_p.at[comp, here], plane_id(peer),
-        )
-
-    def from_p(comp, peer):
-        slot = back_in.at[comp, peer]
-        return copy(slot, slot, send_p.at[comp, peer], recv_p.at[comp, peer], plane_id(peer))
+        return copy(back_out.at[comp, peer], back_in.at[comp, here], EX_P + comp, plane_id(peer))
 
     def to_d(comp, peer):
         return copy(
             field_out.at[comp, lax.div(peer, 2)], field_in.at[comp, here],
-            send_d.at[comp, peer], recv_d.at[comp, here], plane_id(peer),
-        )
-
-    def from_d(comp, peer):
-        slot = field_in.at[comp, peer]
-        return copy(slot, slot, send_d.at[comp, peer], recv_d.at[comp, peer], plane_id(peer))
+            EX_D + comp, plane_id(peer),
+        )
+
+    others, rest = pl.ds(0, PLANE - 1), pl.ds(0, RING - 1)
+
+    def all_of(exchange, comp=0):
+        slots = {
+            EX_A: charge_in,
+            EX_B: modes_in.at[others],
+            EX_Z: spectrum_in.at[rest],
+            EX_C: column_in.at[comp, rest],
+            EX_P: back_in.at[comp, others],
+            EX_D: field_in.at[comp, others],
+        }[exchange]
+        device = ring_id(ring_peer(1)) if exchange in (EX_Z, EX_C) else plane_id(plane_peer(1))
+        return copy(slots, slots, exchange + comp, device)
 
     barrier = pltpu.get_barrier_semaphore()
 
@@ -257,23 +235,13 @@
             result = term if result is None else result + term
         return result
 
-    def send_plane(peer, start):
-        @pl.when(peer != here)
-        def _():
-            start(peer)
-
-    each(0, PLANE, lambda i: from_a(plane_peer(i)).wait_recv())
+    all_of(EX_A).wait_recv()
     load_chunks(charge_in[0] + charge_in[1])
-
-    def row_modes(i):
-        j = lax.rem(tx + 1 + i, BLOCKS)
+    for j in range(BLOCKS):
         modes = transform(j, False)
         modes_out[2 * j] = modes[:, 0:HALF]
         modes_out[2 * j + 1] = modes[:, HALF:TILE]
-        for peer in (2 * j, 2 * j + 1):
-            send_plane(peer, lambda peer: to_b(peer).start())
-
-    each(0, BLOCKS, row_modes)
+    each(1, PLANE, lambda i: to_b(plane_peer(i)).start())
     modes_in[here] = modes_out[here]
 
     first_mode = here * HALF + ty * SHARE
@@ -288,62 +256,47 @@
 
     my_eigen, my_wave = of_mine(EIGEN), of_mine(WAVE)
 
-    each(1, PLANE, lambda i: from_b(plane_peer(i)).wait_recv())
+    all_of(EX_B).wait_recv()
     turned_out[...] = modes_in[...].reshape(TILE, HALF).T.reshape(RING, SHARE, TILE)
     each(1, RING, lambda i: to_z(ring_peer(i)).start())
     spectrum_in[ty] = turned_out[ty]
 
-    each(1, RING, lambda i: from_z(ring_peer(i)).wait_recv())
+    all_of(EX_Z).wait_recv()
     load_chunks(spectrum_in[...])
     scale = f32((2.0 / (GRID + 1)) ** 2)
-
-    def column_modes(j):
+    for j in range(BLOCKS):
         potential = transform(j, False) * scale / (my_eigen + base_ref[j, EIGEN : EIGEN + 1, :])
         scaled[0, j] = -my_wave * potential
         scaled[1, j] = -base_ref[j, WAVE : WAVE + 1, :] * potential
 
-    each(0, BLOCKS, column_modes)
-
     for comp in range(2):
         load_chunks(scaled[comp])
-
-        def column_back(i, comp=comp):
-            j = lax.rem(ty + 1 + i, BLOCKS)
+        for j in range(BLOCKS):
             column_out[comp, j] = transform(j, comp == 1)
-
-            @pl.when(j != ty)
-            def _():
-                to_c(comp, j).start()
-
-        each(0, BLOCKS, column_back)
+        each(1, RING, lambda i, comp=comp: to_c(comp, ring_peer(i)).start())
         column_in[comp, ty] = column_out[comp, ty]
 
     for comp in range(2):
-        each(1, RING, lambda i, comp=comp: from_c(comp, ring_peer(i)).wait_recv())
+        all_of(EX_C, comp).wait_recv()
         back_out[comp] = column_in[comp].reshape(HALF, TILE).T.reshape(PLANE, SHARE, HALF)
         each(1, PLANE, lambda i, comp=comp: to_p(comp, plane_peer(i)).start())
         back_in[comp, here] = back_out[comp, here]
 
     for comp in range(2):
-        each(1, PLANE, lambda i, comp=comp: from_p(comp, plane_peer(i)).wait_recv())
+        all_of(EX_P, comp).wait_recv()
         load_lines(
             jnp.concatenate([back_in[comp, 2 * j] for j in range(BLOCKS)], axis=0),
             jnp.concatenate([back_in[comp, 2 * j + 1] for j in range(BLOCKS)], axis=0),
         )
-
-        def row_back(i, comp=comp):
-            j = lax.rem(tx + 1 + i, BLOCKS)
+        for j in range(BLOCKS):
             field_out[comp, j] = transform(j, comp == 0)
-            for peer in (2 * j, 2 * j + 1):
-                send_plane(peer, lambda peer: to_d(comp, peer).start())
-
-        each(0, BLOCKS, row_back)
+        each(1, PLANE, lambda i, comp=comp: to_d(comp, plane_peer(i)).start())
         field_in[comp, here] = field_out[comp, tx]
 
     loads[4].wait()
     turn = min(SAMPLE_STEP, count)
     for comp in range(2):
-        each(1, PLANE, lambda i, comp=comp: from_d(comp, plane_peer(i)).wait_recv())
+        all_of(EX_D, comp).wait_recv()
         field = field_in[comp].reshape(TILE, TILE)
         field = 0.75 * field + 0.25 * pltpu.roll(field, TILE - 1, 1)
         field = kick_gain * (0.625 * field + 0.375 * pltpu.roll(field, TILE - 1, 0))
@@ -363,13 +316,14 @@
 
         each(0, count // turn, sample)
 
-    each(0, PLANE, lambda i: to_a(plane_peer(i)).wait_send())
-    each(1, PLANE, lambda i: to_b(plane_peer(i)).wait_send())
-    each(1, RING, lambda i: to_z(ring_peer(i)).wait_send())
-    for comp in range(2):
-        each(1, RING, lambda i, comp=comp: to_c(comp, ring_peer(i)).wait_send())
-        each(1, PLANE, lambda i, comp=comp: to_p(comp, plane_peer(i)).wait_send())
-        each(1, PLANE, lambda i, comp=comp: to_d(comp, plane_peer(i)).wait_send())
+    store = pltpu.make_async_copy(out_ref, out_hbm, load.at[0])
+    store.start()
+    for exchange in (EX_A, EX_B, EX_Z):
+        all_of(exchange).wait_send()
+    for comp in range(2):
+        for exchange in (EX_C, EX_P, EX_D):
+            all_of(exchange, comp).wait_send()
+    store.wait()
 
 
 def shards(cell_row, cell_col, weights, momenta):
@@ -380,13 +334,14 @@
         collide_kernel,
         out_shape=jax.ShapeDtypeStruct((2, count), f32),
         in_specs=[pl.BlockSpec(memory_space=pltpu.HBM)] * 5,
-        out_specs=pl.BlockSpec(memory_space=pltpu.VMEM),
+        out_specs=pl.BlockSpec(memory_space=pltpu.HBM),
         scratch_shapes=[
             pltpu.VMEM((1, count), jnp.int32),
             pltpu.VMEM((1, count), jnp.int32),
             pltpu.VMEM((1, count), f32),
             pltpu.VMEM((2, count), f32),
             pltpu.VMEM(base.shape, f32),
+            pltpu.VMEM((2, count), f32),
             pltpu.VMEM((TILE, count), bf16),
             pltpu.VMEM((2 * TILE, TILE), f32),
             pltpu.VMEM((PLANE, SHARE, TILE), f32),
@@ -406,13 +361,7 @@
             pltpu.VMEM((2, BLOCKS, SHARE, TILE), f32),
             pltpu.VMEM((2, PLANE, SHARE, TILE), f32),
             pltpu.VMEM((2 * TILE, TILE), bf16),
-            dma((5,)),
-            dma((PLANE,)), dma((PLANE,)),
-            dma((PLANE,)), dma((PLANE,)),
-            dma((RING,)), dma((RING,)),
-            dma((2, RING)), dma((2, RING)),
-            dma((2, PLANE)), dma((2, PLANE)),
-            dma((2, PLANE)), dma((2, PLANE)),
+            dma((5,)), dma((EXCHANGES,)), dma((EXCHANGES,)),
         ],
         compiler_params=pltpu.CompilerParams(
             vmem_limit_bytes=56 * 1024 * 1024, collective_id=0, has_side_effects=True

time: 66.8 us -> 60.9 us (0.912); the launches traced: 66.5 us -> 59.7 us
  Pallas kernels: 64.9 us -> 58.1 us
    pallas_call x1, Pallas kernels: 64.9 us -> 58.1 us  [shards(): pl.pallas_call(collide_kernel, out_shape=jax.ShapeDtypeStruct((2, count),...]
where the time goes in v3:
time: 60.9 us; the launch traced here: 59.7 us
  Pallas kernels  58.1 us (95%)
  local copies, waits for them, and re-layouts  1.57 us (3%)
    pallas_call x1, Pallas kernels, shards(): pl.pallas_call(collide_kernel, out_shape=jax.ShapeDtypeStruct((2, count),...  58.1 us
    unnamed x1, local copies, waits for them, and re-layouts  1.57 us

profile of v3, /device:TPU:4, one launch (start us, length us, event | category | flops | bytes accessed | tf_op | source)
XLA Modules:
  0.0 59.7 jit_solution(18033153603366625211)
XLA Ops:
  0.0 58.1 %collide.1 = f32[2,16384]{1,0:T(2,128)} custom-call(s32[1,16384]{1,0:T(1,128)} %row_hbm.1, s32[1,16384]{1,0:T(1,128)} %col_hbm.1, f32[1,16384]{1,0:T(1,128)} %weight_hbm.1, f32[2,16384]{1,0:T(2,128)} %bitcast.3, f32[8,72,256]{2,1,0:T(8,128)} %constant.2.clone.base_hbm), custom_call_target="tpu_custom_call" | custom-call | tf_op jit(solution)/shard_map/collide/pallas_call | solution.py:333
  58.1 1.6 %copy.7 = f32[1,2,16384]{2,1,0:T(2,128)} copy(f32[1,2,16384]{2,1,0:T(2,128)} %bitcast.2) | data formatting | bytes 262144

commit v4 on v3

--- a/solution.py
+++ b/solution.py
@@ -55,8 +55,8 @@
 
 
 def collide_kernel(
-    row_hbm, col_hbm, weight_hbm, momenta_hbm, base_hbm, out_hbm,
-    row_ref, col_ref, weight_ref, momenta_ref, base_ref, out_ref,
+    row_hbm, col_hbm, weight_hbm, momenta_hbm, base_hbm, out_ref,
+    row_ref, col_ref, weight_ref, momenta_ref, base_ref,
     on_rows, total, tile_out, tables, even, odd, charge_in, modes_out, modes_in, turned_out,
     spectrum_in, scaled, column_out, column_in, back_out, back_in, field_out, field_in, parts,
     load, sent, came,
@@ -94,11 +94,20 @@
     def ring_id(peer):
         return {"ty": peer}
 
-    def plane_peer(i):
-        return lax.rem(here + i, PLANE)
-
-    def ring_peer(i):
-        return lax.rem(ty + i, RING)
+    def hops(distance, size):
+        return min(distance, size - distance)
+
+    steps = [(dy, dx) for dy in range(4) for dx in range(4)]
+    steps.sort(key=lambda step: -hops(step[0], 4) - hops(step[1], 4))
+    plane_all = [
+        lax.rem(lax.div(here, 4) + dy, 4) * 4 + lax.rem(lax.rem(here, 4) + dx, 4)
+        for dy, dx in steps
+    ]
+    plane_others = plane_all[:-1]
+    ring_others = [
+        lax.rem(ty + step, RING)
+        for step in sorted(range(1, RING), key=lambda step: -hops(step, RING))
+    ]
 
     def copy(src, dst, exchange, device):
         return pltpu.make_async_remote_copy(
@@ -140,7 +149,7 @@
             EX_P: back_in.at[comp, others],
             EX_D: field_in.at[comp, others],
         }[exchange]
-        device = ring_id(ring_peer(1)) if exchange in (EX_Z, EX_C) else plane_id(plane_peer(1))
+        device = ring_id(ring_others[0]) if exchange in (EX_Z, EX_C) else plane_id(plane_others[0])
         return copy(slots, slots, exchange + comp, device)
 
     barrier = pltpu.get_barrier_semaphore()
@@ -150,9 +159,12 @@
             barrier, inc=1, device_id=device, device_id_type=pl.DeviceIdType.MESH
         )
 
-    each(0, PLANE, lambda i: greet(other_id(plane_peer(i))))
-    each(1, PLANE, lambda i: greet(plane_id(plane_peer(i))))
-    each(1, RING, lambda i: greet(ring_id(ring_peer(i))))
+    for peer in plane_all:
+        greet(other_id(peer))
+    for peer in plane_others:
+        greet(plane_id(peer))
+    for peer in ring_others:
+        greet(ring_id(peer))
 
     total[...] = jnp.zeros_like(total)
     for item in loads[0:3]:
@@ -182,7 +194,8 @@
     tile_out[...] = tile.reshape(PLANE, SHARE, TILE)
 
     pl.semaphore_wait(barrier, PLANE + PLANE - 1 + RING - 1)
-    each(0, PLANE, lambda i: to_a(plane_peer(i)).start())
+    for peer in plane_all:
+        to_a(peer).start()
 
     loads[3].wait()
 
@@ -241,7 +254,8 @@
         modes = transform(j, False)
         modes_out[2 * j] = modes[:, 0:HALF]
         modes_out[2 * j + 1] = modes[:, HALF:TILE]
-    each(1, PLANE, lambda i: to_b(plane_peer(i)).start())
+    for peer in plane_others:
+        to_b(peer).start()
     modes_in[here] = modes_out[here]
 
     first_mode = here * HALF + ty * SHARE
@@ -258,7 +272,8 @@
 
     all_of(EX_B).wait_recv()
     turned_out[...] = modes_in[...].reshape(TILE, HALF).T.reshape(RING, SHARE, TILE)
-    each(1, RING, lambda i: to_z(ring_peer(i)).start())
+    for peer in ring_others:
+        to_z(peer).start()
     spectrum_in[ty] = turned_out[ty]
 
     all_of(EX_Z).wait_recv()
@@ -273,13 +288,15 @@
         load_chunks(scaled[comp])
         for j in range(BLOCKS):
             column_out[comp, j] = transform(j, comp == 1)
-        each(1, RING, lambda i, comp=comp: to_c(comp, ring_peer(i)).start())
+        for peer in ring_others:
+            to_c(comp, peer).start()
         column_in[comp, ty] = column_out[comp, ty]
 
     for comp in range(2):
         all_of(EX_C, comp).wait_recv()
         back_out[comp] = column_in[comp].reshape(HALF, TILE).T.reshape(PLANE, SHARE, HALF)
-        each(1, PLANE, lambda i, comp=comp: to_p(comp, plane_peer(i)).start())
+        for peer in plane_others:
+            to_p(comp, peer).start()
         back_in[comp, here] = back_out[comp, here]
 
     for comp in range(2):
@@ -290,7 +307,8 @@
         )
         for j in range(BLOCKS):
             field_out[comp, j] = transform(j, comp == 0)
-        each(1, PLANE, lambda i, comp=comp: to_d(comp, plane_peer(i)).start())
+        for peer in plane_others:
+            to_d(comp, peer).start()
         field_in[comp, here] = field_out[comp, tx]
 
     loads[4].wait()
@@ -316,14 +334,11 @@
 
         each(0, count // turn, sample)
 
-    store = pltpu.make_async_copy(out_ref, out_hbm, load.at[0])
-    store.start()
     for exchange in (EX_A, EX_B, EX_Z):
         all_of(exchange).wait_send()
     for comp in range(2):
         for exchange in (EX_C, EX_P, EX_D):
             all_of(exchange, comp).wait_send()
-    store.wait()
 
 
 def shards(cell_row, cell_col, weights, momenta):
@@ -334,14 +349,13 @@
         collide_kernel,
         out_shape=jax.ShapeDtypeStruct((2, count), f32),
         in_specs=[pl.BlockSpec(memory_space=pltpu.HBM)] * 5,
-        out_specs=pl.BlockSpec(memory_space=pltpu.HBM),
+        out_specs=pl.BlockSpec(memory_space=pltpu.VMEM),
         scratch_shapes=[
             pltpu.VMEM((1, count), jnp.int32),
             pltpu.VMEM((1, count), jnp.int32),
             pltpu.VMEM((1, count), f32),
             pltpu.VMEM((2, count), f32),
             pltpu.VMEM(base.shape, f32),
-            pltpu.VMEM((2, count), f32),
             pltpu.VMEM((TILE, count), bf16),
             pltpu.VMEM((2 * TILE, TILE), f32),
             pltpu.VMEM((PLANE, SHARE, TILE), f32),
@@ -364,10 +378,15 @@
             dma((5,)), dma((EXCHANGES,)), dma((EXCHANGES,)),
         ],
         compiler_params=pltpu.CompilerParams(
-            vmem_limit_bytes=56 * 1024 * 1024, collective_id=0, has_side_effects=True
+            vmem_limit_bytes=48 * 1024 * 1024, collective_id=0, has_side_effects=True
         ),
         name="collide",
-    )(cell_row, cell_col, weights, momenta[0], jnp.asarray(base))
+    )(
+        *[
+            pltpu.with_memory_space_constraint(array, pltpu.HBM)
+            for array in (cell_row, cell_col, weights, momenta[0], jnp.asarray(base))
+        ]
+    )
     return kicked[None]
 
 

time: 60.9 us -> 57.2 us (0.939)
  Pallas kernels: 58.1 us -> 55.7 us
  local copies, waits for them, and re-layouts: 1.57 us -> 0.66 us
    pallas_call x1, Pallas kernels: 58.1 us -> 55.7 us  [shards(): pl.pallas_call(collide_kernel, out_shape=jax.ShapeDtypeStruct((2, count),...]
    unnamed x1, local copies, waits for them, and re-layouts: 1.57 us -> 0.66 us
where the time goes in v4:
time: 57.2 us; the launch traced here: 56.4 us
  Pallas kernels  55.7 us (97%)
  local copies, waits for them, and re-layouts  0.66 us (1%)
    pallas_call x1, Pallas kernels, shards(): pl.pallas_call(collide_kernel, out_shape=jax.ShapeDtypeStruct((2, count),...  55.7 us

profile of v4, /device:TPU:4, one launch (start us, length us, event | category | flops | bytes accessed | tf_op | source)
XLA Modules:
  0.0 56.4 jit_solution(16919718877034789729)
XLA Ops:
  0.0 55.7 %collide.1 = f32[2,16384]{1,0:T(2,128)S(1)} custom-call(s32[1,16384]{1,0:T(1,128)} %row_hbm.1, s32[1,16384]{1,0:T(1,128)} %col_hbm.1, f32[1,16384]{1,0:T(1,128)} %weight_hbm.1, f32[2,16384]{1,0:T(2,128)} %bitcast.3, f32[8,72,256]{2,1,0:T(8,128)} %constant.2.clone.base_hbm), custom_call_target="tpu_custom_call" | custom-call | tf_op jit(solution)/shard_map/collide/pallas_call | solution.py:348
  55.7 0.7 %copy.7 = f32[1,2,16384]{2,1,0:T(2,128)} copy(f32[1,2,16384]{2,1,0:T(2,128)S(1)} %bitcast.2) | data formatting | bytes 262144

commit v5 on v4

--- a/solution.py
+++ b/solution.py
@@ -15,6 +15,7 @@
 HALF = 128
 DEPOSIT_STEP = 8192
 SAMPLE_STEP = 8192
+ONE_HOT_STEP = 4096
 kick_gain = 2.0
 f32 = jnp.float32
 bf16 = jnp.bfloat16
@@ -24,7 +25,7 @@
 )
 BASE_ROWS = 72
 
-EX_A, EX_B, EX_Z, EX_C, EX_P, EX_D, EXCHANGES = 0, 1, 2, 3, 5, 7, 9
+EX_A, EX_B, EX_Z, EX_C, EX_P, EX_D, EX_CELLS, EX_KICK, EXCHANGES = 0, 1, 2, 3, 5, 7, 10, 12, 13
 
 
 def base_tables():
@@ -57,7 +58,7 @@
 def collide_kernel(
     row_hbm, col_hbm, weight_hbm, momenta_hbm, base_hbm, out_ref,
     row_ref, col_ref, weight_ref, momenta_ref, base_ref,
-    on_rows, total, tile_out, tables, even, odd, charge_in, modes_out, modes_in, turned_out,
+    row_two, col_two, kicks_two, kicks_in, rows_two, on_rows, total, tile_out, tables, even, odd, charge_in, modes_out, modes_in, turned_out,
     spectrum_in, scaled, column_out, column_in, back_out, back_in, field_out, field_in, parts,
     load, sent, came,
 ):
@@ -115,8 +116,10 @@
             device_id=device, device_id_type=pl.DeviceIdType.MESH,
         )
 
+    mine_in = dom * BLOCKS + tx
+
     def to_a(peer):
-        return copy(tile_out.at[peer], charge_in.at[dom, tx], EX_A, other_id(peer))
+        return copy(tile_out.at[peer], charge_in.at[mine_in], EX_A, plane_id(peer))
 
     def to_b(peer):
         return copy(modes_out.at[peer], modes_in.at[here], EX_B, plane_id(peer))
@@ -132,22 +135,31 @@
     def to_p(comp, peer):
         return copy(back_out.at[comp, peer], back_in.at[comp, here], EX_P + comp, plane_id(peer))
 
-    def to_d(comp, peer):
+    def to_dx(peer):
+        return copy(field_out.at[0, lax.div(peer, 2)], field_in.at[0, here], EX_D, other_id(peer))
+
+    def to_dy(peer):
         return copy(
-            field_out.at[comp, lax.div(peer, 2)], field_in.at[comp, here],
-            EX_D + comp, plane_id(peer),
-        )
+            field_out.at[1, lax.div(peer, 2)], field_in.at[1 + beam, here],
+            EX_D + 1 + beam, {"beam": jnp.int32(1), **plane_id(peer)},
+        )
+
+    partner = {"beam": 1 - beam}
+    cells_over = [
+        copy(row_ref, row_two, EX_CELLS, partner), copy(col_ref, col_two, EX_CELLS + 1, partner)
+    ]
+    kicks_back = copy(kicks_two, kicks_in, EX_KICK, partner)
 
     others, rest = pl.ds(0, PLANE - 1), pl.ds(0, RING - 1)
 
     def all_of(exchange, comp=0):
         slots = {
-            EX_A: charge_in,
+            EX_A: charge_in.at[others],
             EX_B: modes_in.at[others],
             EX_Z: spectrum_in.at[rest],
             EX_C: column_in.at[comp, rest],
             EX_P: back_in.at[comp, others],
-            EX_D: field_in.at[comp, others],
+            EX_D: field_in.at[comp] if comp < 2 else field_in.at[comp, others],
         }[exchange]
         device = ring_id(ring_others[0]) if exchange in (EX_Z, EX_C) else plane_id(plane_others[0])
         return copy(slots, slots, exchange + comp, device)
@@ -194,8 +206,15 @@
     tile_out[...] = tile.reshape(PLANE, SHARE, TILE)
 
     pl.semaphore_wait(barrier, PLANE + PLANE - 1 + RING - 1)
-    for peer in plane_all:
+    for peer in plane_others:
         to_a(peer).start()
+    charge_in[mine_in] = tile_out[here]
+
+    @pl.when(beam == 0)
+    def _():
+        for item in cells_over:
+            item.start()
+
 
     loads[3].wait()
 
@@ -249,7 +268,7 @@
         return result
 
     all_of(EX_A).wait_recv()
-    load_chunks(charge_in[0] + charge_in[1])
+    load_chunks(charge_in[0:BLOCKS] + charge_in[BLOCKS : 2 * BLOCKS])
     for j in range(BLOCKS):
         modes = transform(j, False)
         modes_out[2 * j] = modes[:, 0:HALF]
@@ -292,6 +311,21 @@
             to_c(comp, peer).start()
         column_in[comp, ty] = column_out[comp, ty]
 
+    wide = min(ONE_HOT_STEP, count)
+
+    def one_hots(i):
+        part = pl.ds(pl.multiple_of(i * wide, wide), wide)
+        cells = lax.broadcasted_iota(jnp.int32, (TILE, wide), 0).astype(f32).astype(bf16)
+        rows_two[:, part] = jnp.where(
+            cells == row_two[:, part].astype(f32).astype(bf16), bf16(1), bf16(0)
+        )
+
+    @pl.when(beam == 1)
+    def _():
+        for item in cells_over:
+            item.wait_recv()
+        each(0, count // wide, one_hots)
+
     for comp in range(2):
         all_of(EX_C, comp).wait_recv()
         back_out[comp] = column_in[comp].reshape(HALF, TILE).T.reshape(PLANE, SHARE, HALF)
@@ -307,37 +341,78 @@
         )
         for j in range(BLOCKS):
             field_out[comp, j] = transform(j, comp == 0)
-        for peer in plane_others:
-            to_d(comp, peer).start()
-        field_in[comp, here] = field_out[comp, tx]
+        if comp == 0:
+            for peer in plane_all:
+                to_dx(peer).start()
+        else:
+            for peer in plane_others:
+                to_dy(peer).start()
+
+    @pl.when(beam == 0)
+    def _():
+        to_dy(here).start()
+
+    @pl.when(beam == 1)
+    def _():
+        field_in[2, here] = field_out[1, tx]
 
     loads[4].wait()
     turn = min(SAMPLE_STEP, count)
-    for comp in range(2):
-        all_of(EX_D, comp).wait_recv()
-        field = field_in[comp].reshape(TILE, TILE)
+
+    def sample(slot, on_rows, cols, store):
+        field = field_in[slot].reshape(TILE, TILE)
         field = 0.75 * field + 0.25 * pltpu.roll(field, TILE - 1, 1)
         field = kick_gain * (0.625 * field + 0.375 * pltpu.roll(field, TILE - 1, 0))
         high, low = split(field)
         parts[0:TILE, :] = high
         parts[TILE : 2 * TILE, :] = low
 
-        def sample(i, comp=comp):
+        def body(i):
             part = pl.ds(pl.multiple_of(i * turn, turn), turn)
             cells = lax.broadcasted_iota(jnp.int32, (TILE, turn), 0)
             near = jnp.dot(parts[...], on_rows[:, part], preferred_element_type=f32)
             near = near[0:TILE] + near[TILE : 2 * TILE]
-            kick = jnp.sum(
-                jnp.where(cells == col_ref[:, part], near, f32(0)), axis=0, keepdims=True
+            store(
+                part,
+                jnp.sum(jnp.where(cells == cols[:, part], near, f32(0)), axis=0, keepdims=True),
             )
+
+        each(0, count // turn, body)
+
+    def own(comp):
+        def store(part, kick):
             out_ref[comp : comp + 1, part] = momenta_ref[comp : comp + 1, part] + kick
 
-        each(0, count // turn, sample)
-
-    for exchange in (EX_A, EX_B, EX_Z):
+        return store
+
+    def for_partner(part, kick):
+        kicks_two[:, part] = kick
+
+    all_of(EX_D).wait_recv()
+    sample(0, on_rows, col_ref, own(0))
+
+    @pl.when(beam == 1)
+    def _():
+        all_of(EX_D, 2).wait_recv()
+        sample(2, rows_two, col_two, for_partner)
+        kicks_back.start()
+        all_of(EX_D, 1).wait_recv()
+        sample(1, on_rows, col_ref, own(1))
+        kicks_back.wait_send()
+        all_of(EX_D, 2).wait_send()
+
+    @pl.when(beam == 0)
+    def _():
+        kicks_back.wait_recv()
+        out_ref[1:2, :] = momenta_ref[1:2, :] + kicks_in[...]
+        for item in cells_over:
+            item.wait_send()
+        all_of(EX_D, 1).wait_send()
+
+    for exchange in (EX_A, EX_B, EX_Z, EX_D):
         all_of(exchange).wait_send()
     for comp in range(2):
-        for exchange in (EX_C, EX_P, EX_D):
+        for exchange in (EX_C, EX_P):
             all_of(exchange, comp).wait_send()
 
 
@@ -356,13 +431,18 @@
             pltpu.VMEM((1, count), f32),
             pltpu.VMEM((2, count), f32),
             pltpu.VMEM(base.shape, f32),
+            pltpu.VMEM((1, count), jnp.int32),
+            pltpu.VMEM((1, count), jnp.int32),
+            pltpu.VMEM((1, count), f32),
+            pltpu.VMEM((1, count), f32),
+            pltpu.VMEM((TILE, count), bf16),
             pltpu.VMEM((TILE, count), bf16),
             pltpu.VMEM((2 * TILE, TILE), f32),
             pltpu.VMEM((PLANE, SHARE, TILE), f32),
             pltpu.VMEM((2, BLOCKS, TILE, TILE), bf16),
             pltpu.VMEM((TILE, TILE), bf16),
             pltpu.VMEM((TILE, TILE), bf16),
-            pltpu.VMEM((2, BLOCKS, SHARE, TILE), f32),
+            pltpu.VMEM((PLANE, SHARE, TILE), f32),
             pltpu.VMEM((PLANE, SHARE, HALF), f32),
             pltpu.VMEM((PLANE, SHARE, HALF), f32),
             pltpu.VMEM((RING, SHARE, TILE), f32),
@@ -373,12 +453,12 @@
             pltpu.VMEM((2, PLANE, SHARE, HALF), f32),
             pltpu.VMEM((2, PLANE, SHARE, HALF), f32),
             pltpu.VMEM((2, BLOCKS, SHARE, TILE), f32),
-            pltpu.VMEM((2, PLANE, SHARE, TILE), f32),
+            pltpu.VMEM((3, PLANE, SHARE, TILE), f32),
             pltpu.VMEM((2 * TILE, TILE), bf16),
             dma((5,)), dma((EXCHANGES,)), dma((EXCHANGES,)),
         ],
         compiler_params=pltpu.CompilerParams(
-            vmem_limit_bytes=48 * 1024 * 1024, collective_id=0, has_side_effects=True
+            vmem_limit_bytes=50 * 1024 * 1024, collective_id=0, has_side_effects=True
         ),
         name="collide",
     )(

time: 57.2 us -> 62.1 us (1.086)
  the two profiles are of different devices: /device:TPU:4 before, /device:TPU:1 now
where the time goes in v5:
time: 62.1 us; the launch traced here: 62 us
  Pallas kernels  61.4 us (99%)
  local copies, waits for them, and re-layouts  0.66 us (1%)
    pallas_call x1, Pallas kernels, shards(): pl.pallas_call(collide_kernel, out_shape=jax.ShapeDtypeStruct((2, count),...  61.4 us

profile of v5, /device:TPU:1, one launch (start us, length us, event | category | flops | bytes accessed | tf_op | source)
XLA Modules:
  0.0 62.0 jit_solution(934472404266806077)
XLA Ops:
  0.0 61.4 %collide.1 = f32[2,16384]{1,0:T(2,128)S(1)} custom-call(s32[1,16384]{1,0:T(1,128)} %row_hbm.1, s32[1,16384]{1,0:T(1,128)} %col_hbm.1, f32[1,16384]{1,0:T(1,128)} %weight_hbm.1, f32[2,16384]{1,0:T(2,128)} %bitcast.3, f32[8,72,256]{2,1,0:T(8,128)} %constant.2.clone.base_hbm), custom_call_target="tpu_custom_call" | custom-call | tf_op jit(solution)/shard_map/collide/pallas_call | solution.py:423
  61.4 0.7 %copy.7 = f32[1,2,16384]{2,1,0:T(2,128)} copy(f32[1,2,16384]{2,1,0:T(2,128)S(1)} %bitcast.2) | data formatting | bytes 262144

commit v6 on v4

--- a/solution.py
+++ b/solution.py
@@ -89,7 +89,7 @@
         return {"tx": lax.div(peer, 2), "dom": lax.rem(peer, 2)}
 
     def other_id(peer):
-        return {"beam": 1 - beam, "tx": lax.div(peer, 2), "dom": lax.rem(peer, 2)}
+        return {"beam": 1 - beam, "ty": peer}
 
     def ring_id(peer):
         return {"ty": peer}
@@ -99,15 +99,15 @@
 
     steps = [(dy, dx) for dy in range(4) for dx in range(4)]
     steps.sort(key=lambda step: -hops(step[0], 4) - hops(step[1], 4))
-    plane_all = [
+    plane_others = [
         lax.rem(lax.div(here, 4) + dy, 4) * 4 + lax.rem(lax.rem(here, 4) + dx, 4)
-        for dy, dx in steps
+        for dy, dx in steps[:-1]
     ]
-    plane_others = plane_all[:-1]
-    ring_others = [
+    ring_all = [
         lax.rem(ty + step, RING)
-        for step in sorted(range(1, RING), key=lambda step: -hops(step, RING))
+        for step in sorted(range(RING), key=lambda step: -hops(step, RING))
     ]
+    ring_others = ring_all[:-1]
 
     def copy(src, dst, exchange, device):
         return pltpu.make_async_remote_copy(
@@ -115,14 +115,16 @@
             device_id=device, device_id_type=pl.DeviceIdType.MESH,
         )
 
+    mine_in = dom * BLOCKS + tx
+
     def to_a(peer):
-        return copy(tile_out.at[peer], charge_in.at[dom, tx], EX_A, other_id(peer))
+        return copy(tile_out.at[peer], charge_in.at[mine_in], EX_A, plane_id(peer))
 
     def to_b(peer):
         return copy(modes_out.at[peer], modes_in.at[here], EX_B, plane_id(peer))
 
     def to_z(peer):
-        return copy(turned_out.at[peer], spectrum_in.at[ty], EX_Z, ring_id(peer))
+        return copy(turned_out.at[peer], spectrum_in.at[ty], EX_Z, other_id(peer))
 
     def to_c(comp, peer):
         return copy(
@@ -142,9 +144,9 @@
 
     def all_of(exchange, comp=0):
         slots = {
-            EX_A: charge_in,
+            EX_A: charge_in.at[others],
             EX_B: modes_in.at[others],
-            EX_Z: spectrum_in.at[rest],
+            EX_Z: spectrum_in,
             EX_C: column_in.at[comp, rest],
             EX_P: back_in.at[comp, others],
             EX_D: field_in.at[comp, others],
@@ -159,7 +161,7 @@
             barrier, inc=1, device_id=device, device_id_type=pl.DeviceIdType.MESH
         )
 
-    for peer in plane_all:
+    for peer in ring_all:
         greet(other_id(peer))
     for peer in plane_others:
         greet(plane_id(peer))
@@ -193,9 +195,10 @@
     tile = 0.625 * tile + 0.375 * pltpu.roll(tile, 1, 0)
     tile_out[...] = tile.reshape(PLANE, SHARE, TILE)
 
-    pl.semaphore_wait(barrier, PLANE + PLANE - 1 + RING - 1)
-    for peer in plane_all:
+    pl.semaphore_wait(barrier, PLANE - 1 + RING + RING - 1)
+    for peer in plane_others:
         to_a(peer).start()
+    charge_in[mine_in] = tile_out[here]
 
     loads[3].wait()
 
@@ -249,7 +252,7 @@
         return result
 
     all_of(EX_A).wait_recv()
-    load_chunks(charge_in[0] + charge_in[1])
+    load_chunks(charge_in[0:BLOCKS] + charge_in[BLOCKS : 2 * BLOCKS])
     for j in range(BLOCKS):
         modes = transform(j, False)
         modes_out[2 * j] = modes[:, 0:HALF]
@@ -272,9 +275,8 @@
 
     all_of(EX_B).wait_recv()
     turned_out[...] = modes_in[...].reshape(TILE, HALF).T.reshape(RING, SHARE, TILE)
-    for peer in ring_others:
+    for peer in ring_all:
         to_z(peer).start()
-    spectrum_in[ty] = turned_out[ty]
 
     all_of(EX_Z).wait_recv()
     load_chunks(spectrum_in[...])
@@ -362,7 +364,7 @@
             pltpu.VMEM((2, BLOCKS, TILE, TILE), bf16),
             pltpu.VMEM((TILE, TILE), bf16),
             pltpu.VMEM((TILE, TILE), bf16),
-            pltpu.VMEM((2, BLOCKS, SHARE, TILE), f32),
+            pltpu.VMEM((PLANE, SHARE, TILE), f32),
             pltpu.VMEM((PLANE, SHARE, HALF), f32),
             pltpu.VMEM((PLANE, SHARE, HALF), f32),
             pltpu.VMEM((RING, SHARE, TILE), f32),

time: 57.2 us -> 57.1 us (level)
  the two profiles are of different devices: /device:TPU:4 before, /device:TPU:1 now
where the time goes in v6:
time: 57.1 us; the launch traced here: 57 us
  Pallas kernels  56.3 us (99%)
  local copies, waits for them, and re-layouts  0.66 us (1%)
    pallas_call x1, Pallas kernels, shards(): pl.pallas_call(collide_kernel, out_shape=jax.ShapeDtypeStruct((2, count),...  56.3 us

profile of v6, /device:TPU:1, one launch (start us, length us, event | category | flops | bytes accessed | tf_op | source)
XLA Modules:
  0.0 57.0 jit_solution(491903372185070758)
XLA Ops:
  0.0 56.3 %collide.1 = f32[2,16384]{1,0:T(2,128)S(1)} custom-call(s32[1,16384]{1,0:T(1,128)} %row_hbm.1, s32[1,16384]{1,0:T(1,128)} %col_hbm.1, f32[1,16384]{1,0:T(1,128)} %weight_hbm.1, f32[2,16384]{1,0:T(2,128)} %bitcast.3, f32[8,72,256]{2,1,0:T(8,128)} %constant.2.clone.base_hbm), custom_call_target="tpu_custom_call" | custom-call | tf_op jit(solution)/shard_map/collide/pallas_call | solution.py:350
  56.3 0.7 %copy.7 = f32[1,2,16384]{2,1,0:T(2,128)} copy(f32[1,2,16384]{2,1,0:T(2,128)S(1)} %bitcast.2) | data formatting | bytes 262144

commit v7 on v4

--- a/solution.py
+++ b/solution.py
@@ -13,7 +13,7 @@
 PLANE = 16
 RING = 8
 HALF = 128
-DEPOSIT_STEP = 8192
+DEPOSIT_STEP = 16384
 SAMPLE_STEP = 8192
 kick_gain = 2.0
 f32 = jnp.float32
@@ -115,11 +115,13 @@
             device_id=device, device_id_type=pl.DeviceIdType.MESH,
         )
 
+    mine_in = dom * BLOCKS + tx
+
     def to_a(peer):
-        return copy(tile_out.at[peer], charge_in.at[dom, tx], EX_A, other_id(peer))
+        return copy(tile_out.at[peer], charge_in.at[mine_in], EX_A, plane_id(peer))
 
     def to_b(peer):
-        return copy(modes_out.at[peer], modes_in.at[here], EX_B, plane_id(peer))
+        return copy(modes_out.at[peer], modes_in.at[here], EX_B, other_id(peer))
 
     def to_z(peer):
         return copy(turned_out.at[peer], spectrum_in.at[ty], EX_Z, ring_id(peer))
@@ -142,8 +144,8 @@
 
     def all_of(exchange, comp=0):
         slots = {
-            EX_A: charge_in,
-            EX_B: modes_in.at[others],
+            EX_A: charge_in.at[others],
+            EX_B: modes_in,
             EX_Z: spectrum_in.at[rest],
             EX_C: column_in.at[comp, rest],
             EX_P: back_in.at[comp, others],
@@ -194,8 +196,9 @@
     tile_out[...] = tile.reshape(PLANE, SHARE, TILE)
 
     pl.semaphore_wait(barrier, PLANE + PLANE - 1 + RING - 1)
-    for peer in plane_all:
+    for peer in plane_others:
         to_a(peer).start()
+    charge_in[mine_in] = tile_out[here]
 
     loads[3].wait()
 
@@ -249,14 +252,13 @@
         return result
 
     all_of(EX_A).wait_recv()
-    load_chunks(charge_in[0] + charge_in[1])
+    load_chunks(charge_in[0:BLOCKS] + charge_in[BLOCKS : 2 * BLOCKS])
     for j in range(BLOCKS):
         modes = transform(j, False)
         modes_out[2 * j] = modes[:, 0:HALF]
         modes_out[2 * j + 1] = modes[:, HALF:TILE]
-    for peer in plane_others:
+    for peer in plane_all:
         to_b(peer).start()
-    modes_in[here] = modes_out[here]
 
     first_mode = here * HALF + ty * SHARE
     lane = lax.broadcasted_iota(jnp.int32, (SHARE, TILE), 1)
@@ -362,7 +364,7 @@
             pltpu.VMEM((2, BLOCKS, TILE, TILE), bf16),
             pltpu.VMEM((TILE, TILE), bf16),
             pltpu.VMEM((TILE, TILE), bf16),
-            pltpu.VMEM((2, BLOCKS, SHARE, TILE), f32),
+            pltpu.VMEM((PLANE, SHARE, TILE), f32),
             pltpu.VMEM((PLANE, SHARE, HALF), f32),
             pltpu.VMEM((PLANE, SHARE, HALF), f32),
             pltpu.VMEM((RING, SHARE, TILE), f32),

time: 57.2 us -> 62.1 us (1.086)
  Pallas kernels: 55.7 us -> 60.9 us
    pallas_call x1, Pallas kernels: 55.7 us -> 60.9 us  [shards(): pl.pallas_call(collide_kernel, out_shape=jax.ShapeDtypeStruct((2, count),...]
where the time goes in v7:
time: 62.1 us; the launch traced here: 61.5 us
  Pallas kernels  60.9 us (98%)
  local copies, waits for them, and re-layouts  0.66 us (1%)
    pallas_call x1, Pallas kernels, shards(): pl.pallas_call(collide_kernel, out_shape=jax.ShapeDtypeStruct((2, count),...  60.9 us

profile of v7, /device:TPU:4, one launch (start us, length us, event | category | flops | bytes accessed | tf_op | source)
XLA Modules:
  0.0 61.5 jit_solution(15289571323944624244)
XLA Ops:
  0.0 60.9 %collide.1 = f32[2,16384]{1,0:T(2,128)S(1)} custom-call(s32[1,16384]{1,0:T(1,128)} %row_hbm.1, s32[1,16384]{1,0:T(1,128)} %col_hbm.1, f32[1,16384]{1,0:T(1,128)} %weight_hbm.1, f32[2,16384]{1,0:T(2,128)} %bitcast.3, f32[8,72,256]{2,1,0:T(8,128)} %constant.2.clone.base_hbm), custom_call_target="tpu_custom_call" | custom-call | tf_op jit(solution)/shard_map/collide/pallas_call | solution.py:350
  60.9 0.7 %copy.7 = f32[1,2,16384]{2,1,0:T(2,128)} copy(f32[1,2,16384]{2,1,0:T(2,128)S(1)} %bitcast.2) | data formatting | bytes 262144

commit v8 on v7

--- a/solution.py
+++ b/solution.py
@@ -13,7 +13,7 @@
 PLANE = 16
 RING = 8
 HALF = 128
-DEPOSIT_STEP = 16384
+DEPOSIT_STEP = 8192
 SAMPLE_STEP = 8192
 kick_gain = 2.0
 f32 = jnp.float32

time: 62.1 us -> 56.7 us (0.913)
  Pallas kernels: 60.9 us -> 55.2 us
    pallas_call x1, Pallas kernels: 60.9 us -> 55.2 us  [shards(): pl.pallas_call(collide_kernel, out_shape=jax.ShapeDtypeStruct((2, count),...]
where the time goes in v8:
time: 56.7 us; the launch traced here: 55.9 us
  Pallas kernels  55.2 us (97%)
  local copies, waits for them, and re-layouts  0.66 us (1%)
    pallas_call x1, Pallas kernels, shards(): pl.pallas_call(collide_kernel, out_shape=jax.ShapeDtypeStruct((2, count),...  55.2 us

profile of v8, /device:TPU:4, one launch (start us, length us, event | category | flops | bytes accessed | tf_op | source)
XLA Modules:
  0.0 55.9 jit_solution(15187383613651313443)
XLA Ops:
  0.0 55.2 %collide.1 = f32[2,16384]{1,0:T(2,128)S(1)} custom-call(s32[1,16384]{1,0:T(1,128)} %row_hbm.1, s32[1,16384]{1,0:T(1,128)} %col_hbm.1, f32[1,16384]{1,0:T(1,128)} %weight_hbm.1, f32[2,16384]{1,0:T(2,128)} %bitcast.3, f32[8,72,256]{2,1,0:T(8,128)} %constant.2.clone.base_hbm), custom_call_target="tpu_custom_call" | custom-call | tf_op jit(solution)/shard_map/collide/pallas_call | solution.py:350
  55.2 0.7 %copy.7 = f32[1,2,16384]{2,1,0:T(2,128)} copy(f32[1,2,16384]{2,1,0:T(2,128)S(1)} %bitcast.2) | data formatting | bytes 262144

commit v9 on v6

--- a/solution.py
+++ b/solution.py
@@ -286,22 +286,24 @@
         scaled[0, j] = -my_wave * potential
         scaled[1, j] = -base_ref[j, WAVE : WAVE + 1, :] * potential
 
-    for comp in range(2):
+    def column_back(comp):
         load_chunks(scaled[comp])
         for j in range(BLOCKS):
             column_out[comp, j] = transform(j, comp == 1)
+
+    def send_c(comp):
         for peer in ring_others:
             to_c(comp, peer).start()
         column_in[comp, ty] = column_out[comp, ty]
 
-    for comp in range(2):
+    def send_p(comp):
         all_of(EX_C, comp).wait_recv()
         back_out[comp] = column_in[comp].reshape(HALF, TILE).T.reshape(PLANE, SHARE, HALF)
         for peer in plane_others:
             to_p(comp, peer).start()
         back_in[comp, here] = back_out[comp, here]
 
-    for comp in range(2):
+    def send_d(comp):
         all_of(EX_P, comp).wait_recv()
         load_lines(
             jnp.concatenate([back_in[comp, 2 * j] for j in range(BLOCKS)], axis=0),
@@ -312,6 +314,15 @@
         for peer in plane_others:
             to_d(comp, peer).start()
         field_in[comp, here] = field_out[comp, tx]
+
+    column_back(0)
+    send_c(0)
+    column_back(1)
+    send_p(0)
+    send_c(1)
+    send_d(0)
+    send_p(1)
+    send_d(1)
 
     loads[4].wait()
     turn = min(SAMPLE_STEP, count)

time: 57.1 us -> 57.9 us (1.014)
  Pallas kernels: 56.3 us -> 57.2 us
    pallas_call x1, Pallas kernels: 56.3 us -> 57.2 us  [shards(): pl.pallas_call(collide_kernel, out_shape=jax.ShapeDtypeStruct((2, count),...]
where the time goes in v9:
time: 57.9 us; the launch traced here: 57.8 us
  Pallas kernels  57.2 us (99%)
  local copies, waits for them, and re-layouts  0.66 us (1%)
    pallas_call x1, Pallas kernels, shards(): pl.pallas_call(collide_kernel, out_shape=jax.ShapeDtypeStruct((2, count),...  57.2 us

profile of v9, /device:TPU:1, one launch (start us, length us, event | category | flops | bytes accessed | tf_op | source)
XLA Modules:
  0.0 57.8 jit_solution(888109948911891836)
XLA Ops:
  0.0 57.2 %collide.1 = f32[2,16384]{1,0:T(2,128)S(1)} custom-call(s32[1,16384]{1,0:T(1,128)} %row_hbm.1, s32[1,16384]{1,0:T(1,128)} %col_hbm.1, f32[1,16384]{1,0:T(1,128)} %weight_hbm.1, f32[2,16384]{1,0:T(2,128)} %bitcast.3, f32[8,72,256]{2,1,0:T(8,128)} %constant.2.clone.base_hbm), custom_call_target="tpu_custom_call" | custom-call | tf_op jit(solution)/shard_map/collide/pallas_call | solution.py:361
  57.2 0.7 %copy.7 = f32[1,2,16384]{2,1,0:T(2,128)} copy(f32[1,2,16384]{2,1,0:T(2,128)S(1)} %bitcast.2) | data formatting | bytes 262144

commit v10 on v8

--- a/solution.py
+++ b/solution.py
@@ -75,7 +75,7 @@
             ]
         )
     ]
-    for item in loads:
+    for item in loads[0:3]:
         item.start()
 
     def each(first, last, act):
@@ -171,6 +171,8 @@
     total[...] = jnp.zeros_like(total)
     for item in loads[0:3]:
         item.wait()
+    for item in loads[3:5]:
+        item.start()
     step = min(DEPOSIT_STEP, count)
 
     def deposit(i):

time: 56.7 us -> 57.8 us (1.019); the launches traced: 55.9 us -> 57.7 us
  Pallas kernels: 55.2 us -> 57 us
    pallas_call x1, Pallas kernels: 55.2 us -> 57 us  [shards(): pl.pallas_call(collide_kernel, out_shape=jax.ShapeDtypeStruct((2, count),...]
where the time goes in v10:
time: 57.8 us; the launch traced here: 57.7 us
  Pallas kernels  57 us (99%)
  local copies, waits for them, and re-layouts  0.66 us (1%)
    pallas_call x1, Pallas kernels, shards(): pl.pallas_call(collide_kernel, out_shape=jax.ShapeDtypeStruct((2, count),...  57 us

profile of v10, /device:TPU:4, one launch (start us, length us, event | category | flops | bytes accessed | tf_op | source)
XLA Modules:
  0.0 57.7 jit_solution(14081596343782447931)
XLA Ops:
  0.0 57.0 %collide.1 = f32[2,16384]{1,0:T(2,128)S(1)} custom-call(s32[1,16384]{1,0:T(1,128)} %row_hbm.1, s32[1,16384]{1,0:T(1,128)} %col_hbm.1, f32[1,16384]{1,0:T(1,128)} %weight_hbm.1, f32[2,16384]{1,0:T(2,128)} %bitcast.3, f32[8,72,256]{2,1,0:T(8,128)} %constant.2.clone.base_hbm), custom_call_target="tpu_custom_call" | custom-call | tf_op jit(solution)/shard_map/collide/pallas_call | solution.py:352
  57.1 0.7 %copy.7 = f32[1,2,16384]{2,1,0:T(2,128)} copy(f32[1,2,16384]{2,1,0:T(2,128)S(1)} %bitcast.2) | data formatting | bytes 262144

commit v11 on v8

--- a/solution.py
+++ b/solution.py
@@ -307,10 +307,20 @@
             jnp.concatenate([back_in[comp, 2 * j] for j in range(BLOCKS)], axis=0),
             jnp.concatenate([back_in[comp, 2 * j + 1] for j in range(BLOCKS)], axis=0),
         )
-        for j in range(BLOCKS):
-            field_out[comp, j] = transform(j, comp == 0)
-        for peer in plane_others:
-            to_d(comp, peer).start()
+        if comp == 0:
+            for half in ((2, 1), (3, 0)):
+                for dy in half:
+                    for low in range(2):
+                        j = lax.rem(lax.div(here, 4) + dy, 4) * 2 + low
+                        field_out[comp, j] = transform(j, True)
+                for step, peer in zip(steps[:-1], plane_others):
+                    if step[0] in half:
+                        to_d(comp, peer).start()
+        else:
+            for j in range(BLOCKS):
+                field_out[comp, j] = transform(j, False)
+            for peer in plane_others:
+                to_d(comp, peer).start()
         field_in[comp, here] = field_out[comp, tx]
 
     loads[4].wait()

time: 56.7 us -> 56.4 us (level)
  no operation moved by 1% of the time
where the time goes in v11:
time: 56.4 us; the launch traced here: 55.7 us
  Pallas kernels  55.1 us (98%)
  local copies, waits for them, and re-layouts  0.66 us (1%)
    pallas_call x1, Pallas kernels, shards(): pl.pallas_call(collide_kernel, out_shape=jax.ShapeDtypeStruct((2, count),...  55.1 us

profile of v11, /device:TPU:4, one launch (start us, length us, event | category | flops | bytes accessed | tf_op | source)
XLA Modules:
  0.0 55.7 jit_solution(11308767422501982568)
XLA Ops:
  0.0 55.1 %collide.1 = f32[2,16384]{1,0:T(2,128)S(1)} custom-call(s32[1,16384]{1,0:T(1,128)} %row_hbm.1, s32[1,16384]{1,0:T(1,128)} %col_hbm.1, f32[1,16384]{1,0:T(1,128)} %weight_hbm.1, f32[2,16384]{1,0:T(2,128)} %bitcast.3, f32[8,72,256]{2,1,0:T(8,128)} %constant.2.clone.base_hbm), custom_call_target="tpu_custom_call" | custom-call | tf_op jit(solution)/shard_map/collide/pallas_call | solution.py:360
  55.1 0.7 %copy.7 = f32[1,2,16384]{2,1,0:T(2,128)} copy(f32[1,2,16384]{2,1,0:T(2,128)S(1)} %bitcast.2) | data formatting | bytes 262144
